TPU v7x, 32 devices: a whole 2x2x4 slice. The times are simulated.
32 devices in a mesh: dp: 2 (over x), ctx: 8 (over z, y), head: 2 (over core).
Axes of the slice: x: 2, y: 2, z: 4, core: 2. Of those that a mesh axis runs over, the one named last changes fastest.
Arguments:
- queries: bfloat16 [2, 1024, 4096], P('dp', 'ctx', 'head'), may hold values from -200 to 200
- targets: bfloat16 [2, 1024, 4096], P('dp', 'ctx', 'head'), may hold values from -3 to 3
- document_keys: bfloat16 [2, 1024, 256], P('dp', 'ctx', 'head'), may hold values from -6 to 6
- document_values: bfloat16 [2, 1024, 256], P('dp', 'ctx', 'head'), may hold values from -6 to 6
- doc_pos: int32 [2, 1024], P('dp', 'ctx'), may hold values from 0 to 1023, each once within a row
- cart_keys: bfloat16 [128, 256], P('ctx', 'head'), may hold values from -8 to 8
- cartridge_values: bfloat16 [128, 256], P('ctx', 'head'), may hold values from -6 to 6
- master: float32 [128, 2, 256], P('ctx', 'head', 'dp'), may hold values from -5 to 5
- first_moment1: float32 [128, 2, 256], P('ctx', 'head', 'dp'), may hold values from -4 to 4
- second_moment2: float32 [128, 2, 256], P('ctx', 'head', 'dp'), may hold values from 0.1 to 2
Outputs:
- new_out: bfloat16 [2, 1024, 4096], P('dp', 'ctx', 'head')
- new_master: float32 [128, 2, 256], P('ctx', 'head', 'dp')
- new_moment1: float32 [128, 2, 256], P('ctx', 'head', 'dp')
- new_moment2: float32 [128, 2, 256], P('ctx', 'head', 'dp')
Inputs may be any that keep to these rules, and one draw needn't show every extreme that they name: Each row of doc_pos holds every position of the document once.
All inputs are finite; a program needn't handle non-finite values.
Results may differ from a plain program's by a relative error of at most 0.015.
Values may be sent and summed in bfloat16 or wider, within the bound.
No kernel may reach another device: no remote copies, remote signals or barrier semaphores. Data moves between devices by JAX's collectives and lax.ppermute only.
A program may use at most 64 MiB of HBM per device.

v0:
```python
import functools
import math

import jax
import jax.numpy as jnp
from jax import lax
from jax.experimental import pallas as pl
from jax.experimental.pallas import tpu as pltpu
from jax.sharding import PartitionSpec as P


beta_one = 0.8
beta_two = 0.95
learn_rate = 0.1
adam_eps = 1e-08
norm_eps = 1e-06
neg_big = -1e30
log2_e = math.log2(math.e)
pos_base = 256.0
f32, bf16 = jnp.float32, jnp.bfloat16


def xor_steps(size):
    assert size & (size - 1) == 0
    return [1 << b for b in reversed(range(size.bit_length() - 1))]


def swap(x, axis, mask, size):
    return lax.ppermute(x, axis, [(i, i ^ mask) for i in range(size)])


def joined(parts):
    return jnp.concatenate(parts, axis=0) if len(parts) > 1 else parts[0]


def spot(chain, axis, mask):
    at = 0
    for n, (name, step) in enumerate(chain):
        if name == axis:
            at = at + (((mask >> (step.bit_length() - 1)) & 1) << n)
    return at


def nt(a, b):
    return lax.dot_general(a, b, (((1,), (1,)), ((), ())), preferred_element_type=f32)


def tn(a, b):
    return lax.dot_general(a, b, (((0,), (0,)), ((), ())), preferred_element_type=f32)


def nn(a, b):
    return jnp.dot(a, b, preferred_element_type=f32)


def pack_kernel(k, v, pos, ck, cv, ma, m1, m2, msg, st, line, sems):
    rows, crows, hd = k.shape[1], ck.shape[0], k.shape[2]
    at = 2 * rows
    copies = [
        (k.at[0], msg.at[0:rows]),
        (v.at[0], msg.at[rows:at]),
        (ck, msg.at[at : at + crows]),
        (cv, msg.at[at + crows : at + 2 * crows]),
        (pos, line),
    ]
    copies += [(ref.at[:, 0, :], st.at[n * crows : (n + 1) * crows]) for n, ref in enumerate((ma, m1, m2))]
    started = [pltpu.make_async_copy(x, y, sems.at[n]) for n, (x, y) in enumerate(copies)]
    for copy in started:
        copy.start()
    for copy in started:
        copy.wait()
    at += 2 * crows
    p = line[...].astype(f32)
    hi = jnp.floor(p * (1.0 / pos_base))
    lo = p - hi * pos_base
    row = lax.broadcasted_iota(jnp.int32, (16, hd), 0)
    both = jnp.where(row == 0, jnp.broadcast_to(hi, (16, hd)), jnp.broadcast_to(lo, (16, hd)))
    msg[at : at + 16] = both.astype(bf16)


def split(refs, stride):
    return [(ref, j * stride) for ref in refs for j in range(ref.shape[0] // stride)]


def positions(ref, at, stride):
    two_rows = ref[at + stride - 16 : at + stride].astype(f32)
    return two_rows[0:1] * pos_base + two_rows[1:2]


def document_part(own, blocks, rows, stride):
    query_pos = jnp.broadcast_to(positions(own, 0, stride), (rows, rows))
    keys, values = [], []
    for ref, at in blocks:
        key_pos = jnp.broadcast_to(positions(ref, at, stride), (rows, rows)).T
        barred = jnp.where(key_pos <= query_pos, 0.0, neg_big).astype(bf16)
        keys.append(jnp.concatenate([ref[at : at + rows], barred], axis=1))
        values.append(ref[at + rows : at + 2 * rows])
    values = jnp.concatenate(values, axis=0)
    return jnp.concatenate(keys, axis=0), jnp.concatenate([values, jnp.ones_like(values)], axis=1)


def heads_of(ref, b, per, hd):
    return jnp.concatenate([ref[:, h * hd : (h + 1) * hd] for h in range(b * per, (b + 1) * per)], axis=0)


def pick(rows, per):
    line = lax.broadcasted_iota(jnp.int32, (rows, rows), 0)
    lane = lax.broadcasted_iota(jnp.int32, (rows, rows), 1)
    one = jnp.where(line == lane, 1.0, 0.0).astype(bf16)
    return jnp.concatenate([one] * per, axis=0)


def wide(x, columns):
    return jnp.concatenate([x] * (columns // x.shape[1]), axis=1)


def attend(qx, part, two, state):
    keys, values = part
    s = nt(qx, keys) * two
    top = jnp.max(s, axis=1, keepdims=True)
    hd = values.shape[1] // 2
    if state is None:
        top = jnp.broadcast_to(top, (s.shape[0], hd))
        both = nn(jnp.exp2(s - wide(top, s.shape[1])).astype(bf16), values)
        return both[:, :hd], both[:, hd:], top
    acc, total, old = state
    top = jnp.maximum(old, top)
    both = nn(jnp.exp2(s - wide(top, s.shape[1])).astype(bf16), values)
    keep = jnp.exp2(old - top)
    return acc * keep + both[:, :hd], total * keep + both[:, hd:], top


def chunk_kernel(n_msgs, scale, per, rows, stride, *refs):
    q, own, msgs = refs[0], refs[1], refs[2 : 2 + n_msgs]
    outs = refs[2 + n_msgs :]
    hd = own.shape[1]
    part = document_part(own, split(msgs, stride), rows, stride)
    eye = pick(rows, per)
    span = per * rows
    for b in range(q.shape[1] // hd // per):
        cut = slice(b * span, (b + 1) * span)
        qx = jnp.concatenate([heads_of(q, b, per, hd), eye], axis=1)
        for ref, x in zip(outs, attend(qx, part, scale * log2_e, None)):
            ref[cut] = x


def gradient_kernel(n_last, masks, scale, per, rows, stride, *refs):
    q, t = refs[:2]
    olds = refs[2:5]
    outs, grad = refs[-4:-1], refs[-1]
    msgs = refs[5:-4]
    own = msgs[0]
    hd = own.shape[1]
    crows = (stride - 2 * rows - 16) // 2
    me = lax.axis_index("ctx")
    two = scale * log2_e
    part = document_part(own, split(msgs[len(msgs) - n_last :], stride), rows, stride)
    every = [(ref, at + 2 * rows) for ref, at in split(msgs, stride)]
    cart_k = jnp.concatenate([ref[at : at + crows] for ref, at in every], axis=0)
    cart_v = jnp.concatenate([ref[at + crows : at + 2 * crows] for ref, at in every], axis=0)
    cart_vx = jnp.concatenate([cart_v, jnp.ones_like(cart_v)], axis=1)
    n_cart = cart_k.shape[0]
    eye = pick(rows, per)
    span = per * rows
    gk = jnp.zeros((n_cart, hd), f32)
    gv = jnp.zeros((n_cart, hd), f32)
    for b in range(q.shape[1] // hd // per):
        cut = slice(b * span, (b + 1) * span)
        qh = heads_of(q, b, per, hd)
        acc, total, top = attend(jnp.concatenate([qh, eye], axis=1), part, two, tuple(ref[cut] for ref in olds))
        for ref, x in zip(outs, (acc, total, top)):
            ref[cut] = x
        sc = nt(qh, cart_k) * two
        both = jnp.maximum(top, jnp.max(sc, axis=1, keepdims=True))
        wc = jnp.exp2(sc - wide(both, n_cart))
        keep = jnp.exp2(top - both)
        more = nn(wc.astype(bf16), cart_vx)
        inv = 1.0 / (total * keep + more[:, hd:])
        out = (acc * keep + more[:, :hd]) * inv
        d_out = out - heads_of(t, b, per, hd).astype(f32)
        delta = jnp.sum(d_out * out, axis=1, keepdims=True)
        d_out_b = d_out.astype(bf16)
        probs = wc * wide(inv, n_cart)
        ds = probs * (nt(d_out_b, cart_v) - delta)
        gk = gk + tn(ds.astype(bf16), qh)
        gv = gv + tn(probs.astype(bf16), d_out_b)
    whole = jnp.concatenate([gk * scale, gv], axis=1).astype(bf16)
    for j, mask in enumerate(masks):
        to = pl.multiple_of((me ^ mask) * crows, crows)
        grad[pl.ds(to, crows)] = whole[j * crows : (j + 1) * crows]


def summed(parts):
    parts = [x.astype(f32) for x in parts]
    if len(parts) == 2:
        return parts[0] + parts[1]
    own, one, two, both = parts
    return (own + both) + (one + two)


def square_kernel(*refs):
    total, squares = refs[-2:]
    g = summed([ref[...] for ref in refs[:-2]])
    total[...] = g
    squares[...] = jnp.broadcast_to(jnp.sum(g * g, keepdims=True), squares.shape)


def update(g, ma, m1, m2):
    one = beta_one * m1 + (1.0 - beta_one) * g
    two = beta_two * m2 + (1.0 - beta_two) * g * g
    return one, two, ma - learn_rate * one / (jnp.sqrt(two) + adam_eps)


def final_kernel(masks, chain, n_dp, scale, per, count, q, acc_in, total_in, top_in, g, sq_a, sq_b, st_near, st_far, *rest):
    rows, hd = q.shape[0], acc_in.shape[1]
    group = q.shape[1] // hd
    crows, width = rest[1].shape[0], rest[1].shape[2]
    me, my_dp = lax.axis_index("ctx"), lax.axis_index("dp")
    two = scale * log2_e
    out_hbm, small_hbm = rest[0], rest[1:4]
    out, small, cart, sems = rest[4], rest[5:8], rest[8], rest[9]
    copies = []

    def send(source, target):
        copies.append(pltpu.make_async_copy(source, target, sems.at[len(copies)]))
        copies[-1].start()

    mean = (sq_a[0:1, 0:1] + sq_b[0:1, 0:1]) * (1.0 / count)
    inv_rms = 1.0 / jnp.sqrt(mean + norm_eps)
    mine = g[pl.ds(pl.multiple_of(me * crows, crows), crows)]
    own = mine[:, 0:width]
    for d in range(1, n_dp):
        own = jnp.where(my_dp == d, mine[:, d * width : (d + 1) * width], own)
    one, sec, new = update(own * inv_rms, *(st_near[n * crows : (n + 1) * crows] for n in range(3)))
    for ref, target, x in zip(small, small_hbm, (new, one, sec)):
        ref[:, 0, :] = x
        send(ref, target)
    for r, mask in enumerate(masks):
        parts = [[], [], []]
        st = st_far if mask & chain[-1][1] else st_near
        for d in range(n_dp):
            at = (spot(chain[:-1], "ctx", mask) + spot(chain[:-1], "dp", my_dp ^ d)) * 3 * crows
            for n in range(3):
                parts[n].append(st[pl.ds(pl.multiple_of(at + n * crows, crows), crows)])
        ma_r, m1_r, m2_r = (jnp.concatenate(x, axis=1) for x in parts)
        rows_g = g[pl.ds(pl.multiple_of((me ^ mask) * crows, crows), crows)]
        _, _, new = update(rows_g * inv_rms, ma_r, m1_r, m2_r)
        cart[r * crows : (r + 1) * crows] = new.astype(bf16)
    cart_k = cart[:, :hd]
    cart_v = cart[:, hd:]
    cart_vx = jnp.concatenate([cart_v, jnp.ones_like(cart_v)], axis=1)
    span = per * rows
    for b in range(group // per):
        heads = range(b * per, (b + 1) * per)
        qh = jnp.concatenate([q[:, h * hd : (h + 1) * hd] for h in heads], axis=0)
        cut = slice(b * span, (b + 1) * span)
        top = top_in[cut]
        sc = nt(qh, cart_k) * two
        both = jnp.maximum(top, jnp.max(sc, axis=1, keepdims=True))
        wc = jnp.exp2(sc - wide(both, sc.shape[1])).astype(bf16)
        keep = jnp.exp2(top - both)
        more = nn(wc, cart_vx)
        res = ((acc_in[cut] * keep + more[:, :hd]) / (total_in[cut] * keep + more[:, hd:])).astype(bf16)
        for n, h in enumerate(heads):
            out[:, h * hd : (h + 1) * hd] = res[n * rows : (n + 1) * rows]
        columns = slice(b * per * hd, (b + 1) * per * hd)
        send(out.at[:, columns], out_hbm.at[:, columns])
    for copy in copies:
        copy.wait()


VMEM = pl.BlockSpec(memory_space=pltpu.VMEM)


def call(body, outs, n_in, scratch=(), limit=40, space=VMEM):
    return pl.pallas_call(
        body,
        out_shape=outs,
        in_specs=[VMEM] * n_in,
        out_specs=tuple(space for _ in outs),
        scratch_shapes=list(scratch),
        compiler_params=pltpu.CompilerParams(vmem_limit_bytes=limit * 2**20),
    )


def local(sizes, queries, targets, document_keys, document_values, doc_pos, cart_keys, cartridge_values, master, first_moment1, second_moment2):
    n_dp, n_ctx, n_head = sizes
    hd = document_keys.shape[2]
    rows = queries.shape[1]
    group = queries.shape[2] // hd
    crows = cart_keys.shape[0]
    scale = hd ** (-0.5)
    steps, dp_steps, head_steps = xor_steps(n_ctx), xor_steps(n_dp), xor_steps(n_head)
    sds = jax.ShapeDtypeStruct
    stride = 2 * rows + 2 * crows + 16
    masks = [0]
    for s in steps:
        masks += [m ^ s for m in masks]
    msg, st = pl.pallas_call(
        pack_kernel,
        out_shape=(sds((stride, hd), bf16), sds((3 * crows, master.shape[2]), f32)),
        in_specs=[pl.BlockSpec(memory_space=pltpu.HBM)] * 8,
        out_specs=(VMEM, VMEM),
        scratch_shapes=[pltpu.VMEM(doc_pos.shape, jnp.int32), pltpu.SemaphoreType.DMA((8,))],
        compiler_params=pltpu.CompilerParams(vmem_limit_bytes=8 * 2**20),
    )(
        *(
            pltpu.with_memory_space_constraint(x, pltpu.HBM)
            for x in (document_keys, document_values, doc_pos, cart_keys, cartridge_values, master, first_moment1, second_moment2)
        )
    )
    q, t = queries[0], targets[0]
    cart = n_ctx * crows
    shapes = (sds((rows * group, hd), f32),) * 3
    last = steps[-1]
    held, fresh, mirrored = [msg], [msg], []
    for s in steps[:-1]:
        older = held[: len(held) - len(fresh)]
        got = [swap(joined(older), "ctx", s, n_ctx)] if older else []
        got.append(swap(joined(fresh), "ctx", s, n_ctx))
        mirrored.append(swap(joined(fresh), "ctx", last, n_ctx))
        held, fresh = held + got, got
    mirrored.append(swap(joined(fresh), "ctx", last, n_ctx))
    msgs = held + mirrored
    body = functools.partial(chunk_kernel, len(msgs) - 1, scale, math.gcd(group, 2), rows, stride)
    state = call(body, shapes, 1 + len(msgs))(q, msg, *msgs[:-1])
    chain = [("ctx", s) for s in steps]
    chain[1:1] = [("dp", s) for s in dp_steps]
    for n, (axis, s) in enumerate(chain):
        if n:
            st = lax.optimization_barrier(jnp.concatenate([st, more], axis=0))
        more = swap(st, axis, s, {"ctx": n_ctx, "dp": n_dp}[axis])
    body = functools.partial(gradient_kernel, 1, masks, scale, math.gcd(group, 16), rows, stride)
    *state, grad = call(body, shapes + (sds((cart, 2 * hd), bf16),), 5 + len(msgs))(q, t, *state, *msgs)
    bits = steps + [s * n_ctx for s in dp_steps]
    rounds = [bits[n : n + 2] for n in range(0, len(bits), 2)]
    for n, pair in enumerate(rounds):
        ways = pair + [sum(pair)] if len(pair) == 2 else pair
        others = [swap(grad, ("dp", "ctx"), m, n_dp * n_ctx) for m in ways]
        if n + 1 < len(rounds):
            grad = summed([grad] + others).astype(bf16)
    total, squares = call(square_kernel, (sds((cart, 2 * hd), f32), sds((8, hd), f32)), 1 + len(others))(grad, *others)
    mine = squares
    theirs = jnp.zeros_like(squares)
    for n, s in enumerate(head_steps):
        if n:
            mine = mine + theirs
        theirs = swap(mine, "head", s, n_head)
    count = master.size * n_dp * n_ctx * n_head
    new_out, new_master, new_m1, new_m2 = call(
        functools.partial(final_kernel, masks, chain, n_dp, scale, math.gcd(group, 8), count),
        (sds((rows, group * hd), bf16),) + (sds(master.shape, f32),) * 3,
        9,
        [pltpu.VMEM((rows, group * hd), bf16)]
        + [pltpu.VMEM(master.shape, f32)] * 3
        + [pltpu.VMEM((cart, 2 * hd), bf16), pltpu.SemaphoreType.DMA((3 + group,))],
        space=pl.BlockSpec(memory_space=pltpu.HBM),
    )(q, *state, total, mine, theirs, st, more)
    return (new_out[None], new_master, new_m1, new_m2)


def solution(mesh):
    in_specs = (
        P("dp", "ctx", "head"),
        P("dp", "ctx", "head"),
        P("dp", "ctx", "head"),
        P("dp", "ctx", "head"),
        P("dp", "ctx"),
        P("ctx", "head"),
        P("ctx", "head"),
        P("ctx", "head", "dp"),
        P("ctx", "head", "dp"),
        P("ctx", "head", "dp"),
    )
    out_specs = (
        P("dp", "ctx", "head"),
        P("ctx", "head", "dp"),
        P("ctx", "head", "dp"),
        P("ctx", "head", "dp"),
    )
    sizes = (mesh.shape["dp"], mesh.shape["ctx"], mesh.shape["head"])

    def step(*args):
        return local(sizes, *args)

    return jax.shard_map(step, mesh=mesh, in_specs=in_specs, out_specs=out_specs, check_vma=False)
```

profile of v0, /device:TPU:0, one launch (start us, length us, event | category | flops | bytes accessed | tf_op | source)
XLA Modules:
  0.0 47.9 jit_solution(15592207387301919547)
XLA Ops:
  0.6 0.0 copy-start
  0.6 0.9 %shard_map.129 = (bf16[304,128]{1,0:T(8,128)(2,1)S(1)}, f32[48,128]{1,0:T(8,128)S(1)}) custom-call(bf16[1,128,128]{2,1,0:T(8,128)(2,1)} %k.1, bf16[1,128,128]{2,1,0:T(8,128)(2,1)} %v.1, s32[1,128]{1,0:T(1,128)} %pos.1, bf16[16,128]{1,0:T(8,128)(2,1)} %ck.1, bf16[16,128]{1,0:T(8,128)(2,1)} %cv.1, f32[16,1,128]{2,1,0:T(1,128)} %ma.1, f32[16,1,128]{2,1,0:T(1,128)} %m1.1, ...), custom_call_target="tpu_custom_call" | custom-call | tf_op jit(solution)/shard_map/pallas_call | solution.py:299
  1.6 4.1 %collective-permute-start = (bf16[304,128]{1,0:T(8,128)(2,1)S(1)}, bf16[304,128]{1,0:T(8,128)(2,1)S(1)}, u32[]{:S(2)}, u32[]{:S(2)}) collective-permute-start(bf16[304,128]{1,0:T(8,128)(2,1)S(1)} %get-tuple-element.19.refs_1_.refs_2_.refs_5_), channel_id=1, source_target_pairs={{0,8},{2,10},{4,12},{6,14},{8,0},{10,2},{12,4},{14,6},{1,9},{3,11}... | collective-permute-start | bytes 233480 | tf_op jit(solution)/shard_map/ppermute | solution.py:29
  5.7 0.1 collective-permute-start.13
  5.8 1.8 %collective-permute-start.1 = (bf16[304,128]{1,0:T(8,128)(2,1)S(1)}, bf16[304,128]{1,0:T(8,128)(2,1)S(1)}, u32[]{:S(2)}, u32[]{:S(2)}) collective-permute-start(bf16[304,128]{1,0:T(8,128)(2,1)S(1)} %get-tuple-element.19.refs_1_.refs_2_.refs_5_), channel_id=1, source_target_pairs={{0,4},{2,6},{4,0},{6,2},{8,12},{10,14},{12,8},{14,10},{1,5},{3,7},... | collective-permute-start | bytes 233480 | tf_op jit(solution)/shard_map/ppermute | solution.py:29
  7.6 2.7 %collective-permute-done.refs_3_.refs_6_ = bf16[304,128]{1,0:T(8,128)(2,1)S(1)} collective-permute-done((bf16[304,128]{1,0:T(8,128)(2,1)S(1)}, bf16[304,128]{1,0:T(8,128)(2,1)S(1)}, u32[]{:S(2)}, u32[]{:S(2)}) %collective-permute-start) | collective-permute-done | bytes 77856 | tf_op jit(solution)/shard_map/ppermute | solution.py:29
  10.3 0.8 %collective-permute-start.2 = (bf16[304,128]{1,0:T(8,128)(2,1)S(1)}, bf16[304,128]{1,0:T(8,128)(2,1)S(1)}, u32[]{:S(2)}, u32[]{:S(2)}) collective-permute-start(bf16[304,128]{1,0:T(8,128)(2,1)S(1)} %collective-permute-done.refs_3_.refs_6_), channel_id=1, source_target_pairs={{0,4},{2,6},{4,0},{6,2},{8,12},{10,14},{12,8},{14,10},{1,5},{3,7},... | collective-permute-start | bytes 233480 | tf_op jit(solution)/shard_map/ppermute | solution.py:29
  11.1 0.0 collective-permute-done.13
  11.1 1.6 %collective-permute-start.14 = (f32[96,128]{1,0:T(8,128)S(1)}, f32[96,128]{1,0:T(8,128)S(1)}, u32[]{:S(2)}, u32[]{:S(2)}) collective-permute-start(f32[96,128]{1,0:T(8,128)S(1)} %pad_maximum_fusion.3), channel_id=1, source_target_pairs={{0,16},{16,0},{1,17},{17,1},{2,18},{18,2},{3,19},{19,3},{4,20},{20... | collective-permute-start | bytes 147464 | tf_op jit(solution)/shard_map/ppermute | solution.py:29
  12.7 0.0 collective-permute-done.1.refs_4_.refs_7_
  12.7 2.0 %collective-permute-done.2.refs_5_.refs_8_ = bf16[304,128]{1,0:T(8,128)(2,1)S(1)} collective-permute-done((bf16[304,128]{1,0:T(8,128)(2,1)S(1)}, bf16[304,128]{1,0:T(8,128)(2,1)S(1)}, u32[]{:S(2)}, u32[]{:S(2)}) %collective-permute-start.2) | collective-permute-done | bytes 77856 | tf_op jit(solution)/shard_map/ppermute | solution.py:29
  14.7 1.8 %collective-permute-start.5 = (bf16[608,128]{1,0:T(8,128)(2,1)S(1)}, bf16[608,128]{1,0:T(8,128)(2,1)S(1)}, u32[]{:S(2)}, u32[]{:S(2)}) collective-permute-start(bf16[608,128]{1,0:T(8,128)(2,1)S(1)} %pad_maximum_fusion.1), channel_id=1, source_target_pairs={{0,2},{2,0},{4,6},{6,4},{8,10},{10,8},{12,14},{14,12},{1,3},{3,1},... | collective-permute-start | bytes 466952 | tf_op jit(solution)/shard_map/ppermute | solution.py:29
  16.5 0.0 collective-permute-done.14
  16.5 0.7 %collective-permute-start.15 = (f32[192,128]{1,0:T(8,128)S(1)}, f32[192,128]{1,0:T(8,128)S(1)}, u32[]{:S(2)}, u32[]{:S(2)}) collective-permute-start(f32[192,128]{1,0:T(8,128)S(1)} %pad_maximum_fusion.2), channel_id=1, source_target_pairs={{0,4},{2,6},{4,0},{6,2},{8,12},{10,14},{12,8},{14,10},{1,5},{3,7},... | collective-permute-start | bytes 294920 | tf_op jit(solution)/shard_map/ppermute | solution.py:29
  17.2 1.1 %collective-permute-start.3 = (bf16[304,128]{1,0:T(8,128)(2,1)S(1)}, bf16[304,128]{1,0:T(8,128)(2,1)S(1)}, u32[]{:S(2)}, u32[]{:S(2)}) collective-permute-start(bf16[304,128]{1,0:T(8,128)(2,1)S(1)} %get-tuple-element.19.refs_1_.refs_2_.refs_5_), channel_id=1, source_target_pairs={{0,2},{2,0},{4,6},{6,4},{8,10},{10,8},{12,14},{14,12},{1,3},{3,1},... | collective-permute-start | bytes 233480 | tf_op jit(solution)/shard_map/ppermute | solution.py:29
  18.3 0.9 %collective-permute-start.4 = (bf16[304,128]{1,0:T(8,128)(2,1)S(1)}, bf16[304,128]{1,0:T(8,128)(2,1)S(1)}, u32[]{:S(2)}, u32[]{:S(2)}) collective-permute-start(bf16[304,128]{1,0:T(8,128)(2,1)S(1)} %collective-permute-done.refs_3_.refs_6_), channel_id=1, source_target_pairs={{0,2},{2,0},{4,6},{6,4},{8,10},{10,8},{12,14},{14,12},{1,3},{3,1},... | collective-permute-start | bytes 233480 | tf_op jit(solution)/shard_map/ppermute | solution.py:29
  19.2 2.8 %collective-permute-done.3.refs_6_.refs_9_ = bf16[304,128]{1,0:T(8,128)(2,1)S(1)} collective-permute-done((bf16[304,128]{1,0:T(8,128)(2,1)S(1)}, bf16[304,128]{1,0:T(8,128)(2,1)S(1)}, u32[]{:S(2)}, u32[]{:S(2)}) %collective-permute-start.3) | collective-permute-done | bytes 77856 | tf_op jit(solution)/shard_map/ppermute | solution.py:29
  22.0 0.8 %collective-permute-done.4.refs_7_.refs_10_ = bf16[304,128]{1,0:T(8,128)(2,1)S(1)} collective-permute-done((bf16[304,128]{1,0:T(8,128)(2,1)S(1)}, bf16[304,128]{1,0:T(8,128)(2,1)S(1)}, u32[]{:S(2)}, u32[]{:S(2)}) %collective-permute-start.4) | collective-permute-done | bytes 77856 | tf_op jit(solution)/shard_map/ppermute | solution.py:29
  22.8 0.0 copy-done
  22.8 0.0 copy-start.1
  22.8 2.5 %shard_map.130 = (f32[2048,128]{1,0:T(8,128)S(1)}, f32[2048,128]{1,0:T(8,128)S(1)}, f32[2048,128]{1,0:T(8,128)S(1)}) custom-call(bf16[128,2048]{1,0:T(8,128)(2,1)S(1)} %bitcast.3, bf16[304,128]{1,0:T(8,128)(2,1)S(1)} %get-tuple-element.19.refs_1_.refs_2_.refs_5_, bf16[304,128]{1,0:T(8,128)(2,1)S(1)} %get-tuple-element.19.refs_1_.refs_2_.refs_5_, ...), custom_call_target="tpu_custom_call" | custom-call | tf_op jit(solution)/shard_map/pallas_call | solution.py:326
  25.3 0.0 collective-permute-done.5.refs_11_
  25.3 0.0 copy-done.1
  25.3 2.7 %shard_map.131 = (f32[2048,128]{1,0:T(8,128)S(1)}, f32[2048,128]{1,0:T(8,128)S(1)}, f32[2048,128]{1,0:T(8,128)S(1)}, bf16[128,256]{1,0:T(8,128)(2,1)S(1)}) custom-call(bf16[128,2048]{1,0:T(8,128)(2,1)S(1)} %bitcast.4, bf16[128,2048]{1,0:T(8,128)(2,1)S(1)} %bitcast.6, f32[2048,128]{1,0:T(8,128)S(1)} %get-tuple-element.20.refs_2_, ...), custom_call_target="tpu_custom_call" | custom-call | tf_op jit(solution)/shard_map/pallas_call | solution.py:334
  28.0 3.6 %collective-permute-start.6 = (bf16[128,256]{1,0:T(8,128)(2,1)S(1)}, bf16[128,256]{1,0:T(8,128)(2,1)S(1)}, u32[]{:S(2)}, u32[]{:S(2)}) collective-permute-start(bf16[128,256]{1,0:T(8,128)(2,1)S(1)} %get-tuple-element.26), channel_id=1, source_target_pairs={{0,12},{2,14},{4,8},{6,10},{8,4},{10,6},{12,0},{14,2},{16,28},{18,... | collective-permute-start | bytes 196616 | tf_op jit(solution)/shard_map/ppermute | solution.py:29
  31.7 0.0 collective-permute-start.7
  31.7 0.8 %collective-permute-start.8 = (bf16[128,256]{1,0:T(8,128)(2,1)S(1)}, bf16[128,256]{1,0:T(8,128)(2,1)S(1)}, u32[]{:S(2)}, u32[]{:S(2)}) collective-permute-start(bf16[128,256]{1,0:T(8,128)(2,1)S(1)} %get-tuple-element.26), channel_id=1, source_target_pairs={{0,4},{2,6},{4,0},{6,2},{8,12},{10,14},{12,8},{14,10},{16,20},{18,... | collective-permute-start | bytes 196616 | tf_op jit(solution)/shard_map/ppermute | solution.py:29
  32.5 0.0 collective-permute-done.15
  32.5 1.4 %collective-permute-start.16 = (f32[384,128]{1,0:T(8,128)S(1)}, f32[384,128]{1,0:T(8,128)S(1)}, u32[]{:S(2)}, u32[]{:S(2)}) collective-permute-start(f32[384,128]{1,0:T(8,128)S(1)} %pad_maximum_fusion.st_near), channel_id=1, source_target_pairs={{0,2},{2,0},{4,6},{6,4},{8,10},{10,8},{12,14},{14,12},{1,3},{3,1},... | collective-permute-start | bytes 589832 | tf_op jit(solution)/shard_map/ppermute | solution.py:29
  33.9 0.5 %collective-permute-done.6 = bf16[128,256]{1,0:T(8,128)(2,1)S(1)} collective-permute-done((bf16[128,256]{1,0:T(8,128)(2,1)S(1)}, bf16[128,256]{1,0:T(8,128)(2,1)S(1)}, u32[]{:S(2)}, u32[]{:S(2)}) %collective-permute-start.6) | collective-permute-done | bytes 65568 | tf_op jit(solution)/shard_map/ppermute | solution.py:29
  34.4 2.6 %collective-permute-done.7 = bf16[128,256]{1,0:T(8,128)(2,1)S(1)} collective-permute-done((bf16[128,256]{1,0:T(8,128)(2,1)S(1)}, bf16[128,256]{1,0:T(8,128)(2,1)S(1)}, u32[]{:S(2)}, u32[]{:S(2)}) %collective-permute-start.7) | collective-permute-done | bytes 65568 | tf_op jit(solution)/shard_map/ppermute | solution.py:29
  37.0 0.0 collective-permute-done.8
  37.1 1.6 %collective-permute-start.10 = (bf16[128,256]{1,0:T(8,128)(2,1)S(1)}, bf16[128,256]{1,0:T(8,128)(2,1)S(1)}, u32[]{:S(2)}, u32[]{:S(2)}) collective-permute-start(bf16[128,256]{1,0:T(8,128)(2,1)S(1)} %add_convert_fusion.refs_0_), channel_id=1, source_target_pairs={{0,16},{2,18},{4,20},{6,22},{8,24},{10,26},{12,28},{14,30},{16,0},... | collective-permute-start | bytes 196616 | tf_op jit(solution)/shard_map/ppermute | solution.py:29
  38.6 1.3 %collective-permute-start.11 = (bf16[128,256]{1,0:T(8,128)(2,1)S(1)}, bf16[128,256]{1,0:T(8,128)(2,1)S(1)}, u32[]{:S(2)}, u32[]{:S(2)}) collective-permute-start(bf16[128,256]{1,0:T(8,128)(2,1)S(1)} %add_convert_fusion.refs_0_), channel_id=1, source_target_pairs={{0,18},{2,16},{4,22},{6,20},{8,26},{10,24},{12,30},{14,28},{16,2},... | collective-permute-start | bytes 196616 | tf_op jit(solution)/shard_map/ppermute | solution.py:29
  39.9 0.7 %collective-permute-start.9 = (bf16[128,256]{1,0:T(8,128)(2,1)S(1)}, bf16[128,256]{1,0:T(8,128)(2,1)S(1)}, u32[]{:S(2)}, u32[]{:S(2)}) collective-permute-start(bf16[128,256]{1,0:T(8,128)(2,1)S(1)} %add_convert_fusion.refs_0_), channel_id=1, source_target_pairs={{0,2},{2,0},{4,6},{6,4},{8,10},{10,8},{12,14},{14,12},{16,18},{18,... | collective-permute-start | bytes 196616 | tf_op jit(solution)/shard_map/ppermute | solution.py:29
  40.6 0.8 %collective-permute-done.10.refs_2_ = bf16[128,256]{1,0:T(8,128)(2,1)S(1)} collective-permute-done((bf16[128,256]{1,0:T(8,128)(2,1)S(1)}, bf16[128,256]{1,0:T(8,128)(2,1)S(1)}, u32[]{:S(2)}, u32[]{:S(2)}) %collective-permute-start.10) | collective-permute-done | bytes 65568 | tf_op jit(solution)/shard_map/ppermute | solution.py:29
  41.4 2.4 %collective-permute-done.11.refs_3_ = bf16[128,256]{1,0:T(8,128)(2,1)S(1)} collective-permute-done((bf16[128,256]{1,0:T(8,128)(2,1)S(1)}, bf16[128,256]{1,0:T(8,128)(2,1)S(1)}, u32[]{:S(2)}, u32[]{:S(2)}) %collective-permute-start.11) | collective-permute-done | bytes 65568 | tf_op jit(solution)/shard_map/ppermute | solution.py:29
  43.8 0.7 %collective-permute-done.9.refs_1_ = bf16[128,256]{1,0:T(8,128)(2,1)S(1)} collective-permute-done((bf16[128,256]{1,0:T(8,128)(2,1)S(1)}, bf16[128,256]{1,0:T(8,128)(2,1)S(1)}, u32[]{:S(2)}, u32[]{:S(2)}) %collective-permute-start.9) | collective-permute-done | bytes 65568 | tf_op jit(solution)/shard_map/ppermute | solution.py:29
  44.5 0.2 shard_map.132
  44.7 0.1 collective-permute-start.12
  44.8 0.0 collective-permute-done.16.st_far
  44.8 1.1 %collective-permute-done.12.sq_b = f32[8,128]{1,0:T(8,128)S(1)} collective-permute-done((f32[8,128]{1,0:T(8,128)S(1)}, f32[8,128]{1,0:T(8,128)S(1)}, u32[]{:S(2)}, u32[]{:S(2)}) %collective-permute-start.12) | collective-permute-done | bytes 4128 | tf_op jit(solution)/shard_map/ppermute | solution.py:29
  45.9 2.0 %shard_map.133 = (bf16[128,2048]{1,0:T(8,128)(2,1)}, f32[16,1,128]{2,1,0:T(1,128)}, f32[16,1,128]{2,1,0:T(1,128)}, f32[16,1,128]{2,1,0:T(1,128)}) custom-call(bf16[128,2048]{1,0:T(8,128)(2,1)S(1)} %bitcast.5, f32[2048,128]{1,0:T(8,128)S(1)} %get-tuple-element.23.acc_in, f32[2048,128]{1,0:T(8,128)S(1)} %get-tuple-element.24.total_in, ...), custom_call_target="tpu_custom_call" | custom-call | tf_op jit(solution)/shard_map/pallas_call | solution.py:350
  (5 shorter events, 0.1 us)
Async XLA Ops:
  0.6 22.2 %copy-start = (bf16[1,128,2048]{2,1,0:T(8,128)(2,1)S(1)}, bf16[1,128,2048]{2,1,0:T(8,128)(2,1)}, u32[]{:S(2)}) copy-start(bf16[1,128,2048]{2,1,0:T(8,128)(2,1)} %param.10) | copy-start | bytes 1572868
  1.6 8.7 %collective-permute-start = (bf16[304,128]{1,0:T(8,128)(2,1)S(1)}, bf16[304,128]{1,0:T(8,128)(2,1)S(1)}, u32[]{:S(2)}, u32[]{:S(2)}) collective-permute-start(bf16[304,128]{1,0:T(8,128)(2,1)S(1)} %get-tuple-element.19.refs_1_.refs_2_.refs_5_), channel_id=1, source_target_pairs={{0,8},{2,10},{4,12},{6,14},{8,0},{10,2},{12,4},{14,6},{1,9},{3,11}... | collective-permute-start | bytes 233480 | tf_op jit(solution)/shard_map/ppermute | solution.py:29
  5.7 5.4 %collective-permute-start.13 = (f32[48,128]{1,0:T(8,128)S(1)}, f32[48,128]{1,0:T(8,128)S(1)}, u32[]{:S(2)}, u32[]{:S(2)}) collective-permute-start(f32[48,128]{1,0:T(8,128)S(1)} %get-tuple-element.29), channel_id=1, source_target_pairs={{0,8},{2,10},{4,12},{6,14},{8,0},{10,2},{12,4},{14,6},{1,9},{3,11}... | collective-permute-start | bytes 73736 | tf_op jit(solution)/shard_map/ppermute | solution.py:29
  5.8 6.8 %collective-permute-start.1 = (bf16[304,128]{1,0:T(8,128)(2,1)S(1)}, bf16[304,128]{1,0:T(8,128)(2,1)S(1)}, u32[]{:S(2)}, u32[]{:S(2)}) collective-permute-start(bf16[304,128]{1,0:T(8,128)(2,1)S(1)} %get-tuple-element.19.refs_1_.refs_2_.refs_5_), channel_id=1, source_target_pairs={{0,4},{2,6},{4,0},{6,2},{8,12},{10,14},{12,8},{14,10},{1,5},{3,7},... | collective-permute-start | bytes 233480 | tf_op jit(solution)/shard_map/ppermute | solution.py:29
  10.3 4.4 %collective-permute-start.2 = (bf16[304,128]{1,0:T(8,128)(2,1)S(1)}, bf16[304,128]{1,0:T(8,128)(2,1)S(1)}, u32[]{:S(2)}, u32[]{:S(2)}) collective-permute-start(bf16[304,128]{1,0:T(8,128)(2,1)S(1)} %collective-permute-done.refs_3_.refs_6_), channel_id=1, source_target_pairs={{0,4},{2,6},{4,0},{6,2},{8,12},{10,14},{12,8},{14,10},{1,5},{3,7},... | collective-permute-start | bytes 233480 | tf_op jit(solution)/shard_map/ppermute | solution.py:29
  11.1 5.4 %collective-permute-start.14 = (f32[96,128]{1,0:T(8,128)S(1)}, f32[96,128]{1,0:T(8,128)S(1)}, u32[]{:S(2)}, u32[]{:S(2)}) collective-permute-start(f32[96,128]{1,0:T(8,128)S(1)} %pad_maximum_fusion.3), channel_id=1, source_target_pairs={{0,16},{16,0},{1,17},{17,1},{2,18},{18,2},{3,19},{19,3},{4,20},{20... | collective-permute-start | bytes 147464 | tf_op jit(solution)/shard_map/ppermute | solution.py:29
  14.7 10.6 %collective-permute-start.5 = (bf16[608,128]{1,0:T(8,128)(2,1)S(1)}, bf16[608,128]{1,0:T(8,128)(2,1)S(1)}, u32[]{:S(2)}, u32[]{:S(2)}) collective-permute-start(bf16[608,128]{1,0:T(8,128)(2,1)S(1)} %pad_maximum_fusion.1), channel_id=1, source_target_pairs={{0,2},{2,0},{4,6},{6,4},{8,10},{10,8},{12,14},{14,12},{1,3},{3,1},... | collective-permute-start | bytes 466952 | tf_op jit(solution)/shard_map/ppermute | solution.py:29
  16.5 16.0 %collective-permute-start.15 = (f32[192,128]{1,0:T(8,128)S(1)}, f32[192,128]{1,0:T(8,128)S(1)}, u32[]{:S(2)}, u32[]{:S(2)}) collective-permute-start(f32[192,128]{1,0:T(8,128)S(1)} %pad_maximum_fusion.2), channel_id=1, source_target_pairs={{0,4},{2,6},{4,0},{6,2},{8,12},{10,14},{12,8},{14,10},{1,5},{3,7},... | collective-permute-start | bytes 294920 | tf_op jit(solution)/shard_map/ppermute | solution.py:29
  17.2 4.8 %collective-permute-start.3 = (bf16[304,128]{1,0:T(8,128)(2,1)S(1)}, bf16[304,128]{1,0:T(8,128)(2,1)S(1)}, u32[]{:S(2)}, u32[]{:S(2)}) collective-permute-start(bf16[304,128]{1,0:T(8,128)(2,1)S(1)} %get-tuple-element.19.refs_1_.refs_2_.refs_5_), channel_id=1, source_target_pairs={{0,2},{2,0},{4,6},{6,4},{8,10},{10,8},{12,14},{14,12},{1,3},{3,1},... | collective-permute-start | bytes 233480 | tf_op jit(solution)/shard_map/ppermute | solution.py:29
  18.3 4.6 %collective-permute-start.4 = (bf16[304,128]{1,0:T(8,128)(2,1)S(1)}, bf16[304,128]{1,0:T(8,128)(2,1)S(1)}, u32[]{:S(2)}, u32[]{:S(2)}) collective-permute-start(bf16[304,128]{1,0:T(8,128)(2,1)S(1)} %collective-permute-done.refs_3_.refs_6_), channel_id=1, source_target_pairs={{0,2},{2,0},{4,6},{6,4},{8,10},{10,8},{12,14},{14,12},{1,3},{3,1},... | collective-permute-start | bytes 233480 | tf_op jit(solution)/shard_map/ppermute | solution.py:29
  22.8 2.5 %copy-start.1 = (bf16[1,128,2048]{2,1,0:T(8,128)(2,1)S(1)}, bf16[1,128,2048]{2,1,0:T(8,128)(2,1)}, u32[]{:S(2)}) copy-start(bf16[1,128,2048]{2,1,0:T(8,128)(2,1)} %param.11) | copy-start | bytes 1572868
  28.0 6.4 %collective-permute-start.6 = (bf16[128,256]{1,0:T(8,128)(2,1)S(1)}, bf16[128,256]{1,0:T(8,128)(2,1)S(1)}, u32[]{:S(2)}, u32[]{:S(2)}) collective-permute-start(bf16[128,256]{1,0:T(8,128)(2,1)S(1)} %get-tuple-element.26), channel_id=1, source_target_pairs={{0,12},{2,14},{4,8},{6,10},{8,4},{10,6},{12,0},{14,2},{16,28},{18,... | collective-permute-start | bytes 196616 | tf_op jit(solution)/shard_map/ppermute | solution.py:29
  31.7 5.3 %collective-permute-start.7 = (bf16[128,256]{1,0:T(8,128)(2,1)S(1)}, bf16[128,256]{1,0:T(8,128)(2,1)S(1)}, u32[]{:S(2)}, u32[]{:S(2)}) collective-permute-start(bf16[128,256]{1,0:T(8,128)(2,1)S(1)} %get-tuple-element.26), channel_id=1, source_target_pairs={{0,8},{2,10},{4,12},{6,14},{8,0},{10,2},{12,4},{14,6},{16,24},{18,... | collective-permute-start | bytes 196616 | tf_op jit(solution)/shard_map/ppermute | solution.py:29
  31.7 5.3 %collective-permute-start.8 = (bf16[128,256]{1,0:T(8,128)(2,1)S(1)}, bf16[128,256]{1,0:T(8,128)(2,1)S(1)}, u32[]{:S(2)}, u32[]{:S(2)}) collective-permute-start(bf16[128,256]{1,0:T(8,128)(2,1)S(1)} %get-tuple-element.26), channel_id=1, source_target_pairs={{0,4},{2,6},{4,0},{6,2},{8,12},{10,14},{12,8},{14,10},{16,20},{18,... | collective-permute-start | bytes 196616 | tf_op jit(solution)/shard_map/ppermute | solution.py:29
  32.5 12.2 %collective-permute-start.16 = (f32[384,128]{1,0:T(8,128)S(1)}, f32[384,128]{1,0:T(8,128)S(1)}, u32[]{:S(2)}, u32[]{:S(2)}) collective-permute-start(f32[384,128]{1,0:T(8,128)S(1)} %pad_maximum_fusion.st_near), channel_id=1, source_target_pairs={{0,2},{2,0},{4,6},{6,4},{8,10},{10,8},{12,14},{14,12},{1,3},{3,1},... | collective-permute-start | bytes 589832 | tf_op jit(solution)/shard_map/ppermute | solution.py:29
  37.1 4.3 %collective-permute-start.10 = (bf16[128,256]{1,0:T(8,128)(2,1)S(1)}, bf16[128,256]{1,0:T(8,128)(2,1)S(1)}, u32[]{:S(2)}, u32[]{:S(2)}) collective-permute-start(bf16[128,256]{1,0:T(8,128)(2,1)S(1)} %add_convert_fusion.refs_0_), channel_id=1, source_target_pairs={{0,16},{2,18},{4,20},{6,22},{8,24},{10,26},{12,28},{14,30},{16,0},... | collective-permute-start | bytes 196616 | tf_op jit(solution)/shard_map/ppermute | solution.py:29
  38.6 5.2 %collective-permute-start.11 = (bf16[128,256]{1,0:T(8,128)(2,1)S(1)}, bf16[128,256]{1,0:T(8,128)(2,1)S(1)}, u32[]{:S(2)}, u32[]{:S(2)}) collective-permute-start(bf16[128,256]{1,0:T(8,128)(2,1)S(1)} %add_convert_fusion.refs_0_), channel_id=1, source_target_pairs={{0,18},{2,16},{4,22},{6,20},{8,26},{10,24},{12,30},{14,28},{16,2},... | collective-permute-start | bytes 196616 | tf_op jit(solution)/shard_map/ppermute | solution.py:29
  39.9 4.5 %collective-permute-start.9 = (bf16[128,256]{1,0:T(8,128)(2,1)S(1)}, bf16[128,256]{1,0:T(8,128)(2,1)S(1)}, u32[]{:S(2)}, u32[]{:S(2)}) collective-permute-start(bf16[128,256]{1,0:T(8,128)(2,1)S(1)} %add_convert_fusion.refs_0_), channel_id=1, source_target_pairs={{0,2},{2,0},{4,6},{6,4},{8,10},{10,8},{12,14},{14,12},{16,18},{18,... | collective-permute-start | bytes 196616 | tf_op jit(solution)/shard_map/ppermute | solution.py:29
  44.7 1.2 %collective-permute-start.12 = (f32[8,128]{1,0:T(8,128)S(1)}, f32[8,128]{1,0:T(8,128)S(1)}, u32[]{:S(2)}, u32[]{:S(2)}) collective-permute-start(f32[8,128]{1,0:T(8,128)S(1)} %get-tuple-element.28.sq_a), channel_id=1, source_target_pairs={{0,1},{1,0},{2,3},{3,2},{4,5},{5,4},{6,7},{7,6},{8,9},{9,8},{10,11... | collective-permute-start | bytes 12296 | tf_op jit(solution)/shard_map/ppermute | solution.py:29
where the time goes:
time: 48.1 us; the launch traced here: 47.9 us
  starting transfers between devices  22.3 us (46%)
  waiting for transfers between devices  16.4 us (34%)
  Pallas kernels  8.3 us (17%)
  between operations  0.73 us (2%)
    ppermute x17, starting transfers between devices, swap(): return lax.ppermute(x, axis, [(i, i ^ mask) for i in range(size)])  22.3 us
    ppermute x17, waiting for transfers between devices, swap(): return lax.ppermute(x, axis, [(i, i ^ mask) for i in range(size)])  16.4 us
    pallas_call x1, Pallas kernels, local(): call(body, shapes + (sds((cart, 2 * hd), bf16),), 5 + len(msgs))  2.69 us
    pallas_call x1, Pallas kernels, local(): state = call(body, shapes, 1 + len(msgs))(q, msg, *msgs[:-1])  2.47 us
    pallas_call x1, Pallas kernels, local(): call(functools.partial(final_kernel, masks, chain, n_dp, scale, math.gcd(...  2 us
  transfers between devices with their start and end apart: 17, of which 10 were waited for; matrix products, arithmetic and copies ran while one was open for 0% of the time, Pallas kernels for 11%

commit v1 on v0

--- a/solution.py
+++ b/solution.py
@@ -53,7 +53,7 @@
     return jnp.dot(a, b, preferred_element_type=f32)
 
 
-def pack_kernel(k, v, pos, ck, cv, ma, m1, m2, msg, st, line, sems):
+def pack_kernel(k, v, pos, ck, cv, ma, m1, m2, q, msg, st, q_here, line, sems):
     rows, crows, hd = k.shape[1], ck.shape[0], k.shape[2]
     at = 2 * rows
     copies = [
@@ -64,6 +64,7 @@
         (pos, line),
     ]
     copies += [(ref.at[:, 0, :], st.at[n * crows : (n + 1) * crows]) for n, ref in enumerate((ma, m1, m2))]
+    copies.append((q.at[0], q_here))
     started = [pltpu.make_async_copy(x, y, sems.at[n]) for n, (x, y) in enumerate(copies)]
     for copy in started:
         copy.start()
@@ -130,21 +131,23 @@
     return acc * keep + both[:, :hd], total * keep + both[:, hd:], top
 
 
-def chunk_kernel(n_msgs, scale, per, rows, stride, *refs):
+def chunk_kernel(skipped, n_msgs, scale, per, rows, stride, *refs):
     q, own, msgs = refs[0], refs[1], refs[2 : 2 + n_msgs]
-    outs = refs[2 + n_msgs :]
+    olds, outs = refs[2 + n_msgs : -3], refs[-3:]
     hd = own.shape[1]
-    part = document_part(own, split(msgs, stride), rows, stride)
+    blocks = split(msgs, stride)
+    part = document_part(own, blocks[: len(blocks) - skipped], rows, stride)
     eye = pick(rows, per)
     span = per * rows
     for b in range(q.shape[1] // hd // per):
         cut = slice(b * span, (b + 1) * span)
         qx = jnp.concatenate([heads_of(q, b, per, hd), eye], axis=1)
-        for ref, x in zip(outs, attend(qx, part, scale * log2_e, None)):
+        state = tuple(ref[cut] for ref in olds) if olds else None
+        for ref, x in zip(outs, attend(qx, part, scale * log2_e, state)):
             ref[cut] = x
 
 
-def gradient_kernel(n_last, masks, scale, per, rows, stride, *refs):
+def gradient_kernel(first_blocks, masks, scale, per, rows, stride, *refs):
     q, t = refs[:2]
     olds = refs[2:5]
     outs, grad = refs[-4:-1], refs[-1]
@@ -154,7 +157,7 @@
     crows = (stride - 2 * rows - 16) // 2
     me = lax.axis_index("ctx")
     two = scale * log2_e
-    part = document_part(own, split(msgs[len(msgs) - n_last :], stride), rows, stride)
+    part = document_part(own, split(msgs, stride)[first_blocks:], rows, stride)
     every = [(ref, at + 2 * rows) for ref, at in split(msgs, stride)]
     cart_k = jnp.concatenate([ref[at : at + crows] for ref, at in every], axis=0)
     cart_v = jnp.concatenate([ref[at + crows : at + 2 * crows] for ref, at in every], axis=0)
@@ -296,41 +299,49 @@
     masks = [0]
     for s in steps:
         masks += [m ^ s for m in masks]
-    msg, st = pl.pallas_call(
+    msg, st, q = pl.pallas_call(
         pack_kernel,
-        out_shape=(sds((stride, hd), bf16), sds((3 * crows, master.shape[2]), f32)),
-        in_specs=[pl.BlockSpec(memory_space=pltpu.HBM)] * 8,
-        out_specs=(VMEM, VMEM),
-        scratch_shapes=[pltpu.VMEM(doc_pos.shape, jnp.int32), pltpu.SemaphoreType.DMA((8,))],
+        out_shape=(sds((stride, hd), bf16), sds((3 * crows, master.shape[2]), f32), sds(queries.shape[1:], queries.dtype)),
+        in_specs=[pl.BlockSpec(memory_space=pltpu.HBM)] * 9,
+        out_specs=(VMEM, VMEM, VMEM),
+        scratch_shapes=[pltpu.VMEM(doc_pos.shape, jnp.int32), pltpu.SemaphoreType.DMA((9,))],
         compiler_params=pltpu.CompilerParams(vmem_limit_bytes=8 * 2**20),
     )(
         *(
             pltpu.with_memory_space_constraint(x, pltpu.HBM)
-            for x in (document_keys, document_values, doc_pos, cart_keys, cartridge_values, master, first_moment1, second_moment2)
+            for x in (document_keys, document_values, doc_pos, cart_keys, cartridge_values, master, first_moment1, second_moment2, queries)
         )
     )
-    q, t = queries[0], targets[0]
+    t = targets[0]
     cart = n_ctx * crows
     shapes = (sds((rows * group, hd), f32),) * 3
     last = steps[-1]
-    held, fresh, mirrored = [msg], [msg], []
+    held, fresh, unsent, mirrored = [msg], [msg], [msg], []
     for s in steps[:-1]:
         older = held[: len(held) - len(fresh)]
-        got = [swap(joined(older), "ctx", s, n_ctx)] if older else []
-        got.append(swap(joined(fresh), "ctx", s, n_ctx))
-        mirrored.append(swap(joined(fresh), "ctx", last, n_ctx))
-        held, fresh = held + got, got
-    mirrored.append(swap(joined(fresh), "ctx", last, n_ctx))
+        early = [swap(joined(older), "ctx", s, n_ctx)] if older else []
+        newest = [swap(joined(fresh), "ctx", s, n_ctx)]
+        mirrored.append(swap(joined(unsent + early), "ctx", last, n_ctx))
+        fresh, unsent = early + newest, newest
+        held = held + fresh
+    mirrored.append(swap(joined(unsent), "ctx", last, n_ctx))
     msgs = held + mirrored
-    body = functools.partial(chunk_kernel, len(msgs) - 1, scale, math.gcd(group, 2), rows, stride)
-    state = call(body, shapes, 1 + len(msgs))(q, msg, *msgs[:-1])
+    tail = mirrored[-1].shape[0] // stride
+    left = max(2, tail)
+
+    def document(some, skipped, state):
+        body = functools.partial(chunk_kernel, skipped, len(some), scale, math.gcd(group, 2), rows, stride)
+        return call(body, shapes, 2 + len(some) + len(state))(q, msg, *some, *state)
+
+    state = document(held[:-1] + mirrored[:-2], 0, ())
+    state = document(held[-1:] + mirrored[-2:-1], left - tail, state)
     chain = [("ctx", s) for s in steps]
     chain[1:1] = [("dp", s) for s in dp_steps]
     for n, (axis, s) in enumerate(chain):
         if n:
             st = lax.optimization_barrier(jnp.concatenate([st, more], axis=0))
         more = swap(st, axis, s, {"ctx": n_ctx, "dp": n_dp}[axis])
-    body = functools.partial(gradient_kernel, 1, masks, scale, math.gcd(group, 16), rows, stride)
+    body = functools.partial(gradient_kernel, n_ctx - left, masks, scale, math.gcd(group, 16), rows, stride)
     *state, grad = call(body, shapes + (sds((cart, 2 * hd), bf16),), 5 + len(msgs))(q, t, *state, *msgs)
     bits = steps + [s * n_ctx for s in dp_steps]
     rounds = [bits[n : n + 2] for n in range(0, len(bits), 2)]

time: 48.1 us -> 45.8 us (0.952)
  waiting for transfers between devices: 16.4 us -> 14 us
  Pallas kernels: 8.3 us -> 9.06 us
  starting transfers between devices: 22.3 us -> 21.7 us
    ppermute x17, waiting for transfers between devices: 16.4 us -> 14 us  [swap(): return lax.ppermute(x, axis, [(i, i ^ mask) for i in range(size)])]
    ppermute x17, starting transfers between devices: 22.3 us -> 21.7 us  [swap(): return lax.ppermute(x, axis, [(i, i ^ mask) for i in range(size)])]
    pallas_call x1 -> x2, Pallas kernels: 2.47 us -> 3.03 us  [document(): return call(body, shapes, 2 + len(some) + len(state))(q, msg, *some, *state)]
  transfers between devices with their start and end apart: 17 -> 17, of which waited for: 10 -> 9; matrix products, arithmetic and copies ran while one was open for 0% -> 0% of each run, Pallas kernels for 11% -> 13%
where the time goes in v1:
time: 45.8 us; the launch traced here: 45.6 us
  starting transfers between devices  21.7 us (47%)
  waiting for transfers between devices  14 us (31%)
  Pallas kernels  9.06 us (20%)
  between operations  0.74 us (2%)
    ppermute x17, starting transfers between devices, swap(): return lax.ppermute(x, axis, [(i, i ^ mask) for i in range(size)])  21.7 us
    ppermute x17, waiting for transfers between devices, swap(): return lax.ppermute(x, axis, [(i, i ^ mask) for i in range(size)])  14 us
    pallas_call x2, Pallas kernels, document(): return call(body, shapes, 2 + len(some) + len(state))(q, msg, *some, *state)  3.03 us
    pallas_call x1, Pallas kernels, local(): call(body, shapes + (sds((cart, 2 * hd), bf16),), 5 + len(msgs))  2.57 us
    pallas_call x1, Pallas kernels, local(): call(functools.partial(final_kernel, masks, chain, n_dp, scale, math.gcd(...  2 us
    pallas_call x1, Pallas kernels, local(): pl.pallas_call(pack_kernel, out_shape=(sds((stride, hd), bf16), sds((3 *...  1.27 us
  transfers between devices with their start and end apart: 17, of which 9 were waited for; matrix products, arithmetic and copies ran while one was open for 0% of the time, Pallas kernels for 13%

profile of v1, /device:TPU:0, one launch (start us, length us, event | category | flops | bytes accessed | tf_op | source)
XLA Modules:
  0.0 45.6 jit_solution(572893600321180859)
XLA Ops:
  0.6 1.3 %shard_map.129 = (bf16[304,128]{1,0:T(8,128)(2,1)S(1)}, f32[48,128]{1,0:T(8,128)S(1)}, bf16[128,2048]{1,0:T(8,128)(2,1)S(1)}) custom-call(bf16[1,128,128]{2,1,0:T(8,128)(2,1)} %k.1, bf16[1,128,128]{2,1,0:T(8,128)(2,1)} %v.1, s32[1,128]{1,0:T(1,128)} %pos.1, bf16[16,128]{1,0:T(8,128)(2,1)} %ck.1, bf16[16,128]{1,0:T(8,128)(2,1)} %cv.1, f32[16,1,128]{2,1,0:T(1,128)} %ma.1, ...), custom_call_target="tpu_custom_call" | custom-call | tf_op jit(solution)/shard_map/pallas_call | solution.py:302
  1.9 4.1 %collective-permute-start.13 = (f32[48,128]{1,0:T(8,128)S(1)}, f32[48,128]{1,0:T(8,128)S(1)}, u32[]{:S(2)}, u32[]{:S(2)}) collective-permute-start(f32[48,128]{1,0:T(8,128)S(1)} %get-tuple-element.37), channel_id=1, source_target_pairs={{0,8},{2,10},{4,12},{6,14},{8,0},{10,2},{12,4},{14,6},{1,9},{3,11}... | collective-permute-start | bytes 73736 | tf_op jit(solution)/shard_map/ppermute | solution.py:29
  6.0 0.1 collective-permute-start
  6.1 1.8 %collective-permute-start.2 = (bf16[304,128]{1,0:T(8,128)(2,1)S(1)}, bf16[304,128]{1,0:T(8,128)(2,1)S(1)}, u32[]{:S(2)}, u32[]{:S(2)}) collective-permute-start(bf16[304,128]{1,0:T(8,128)(2,1)S(1)} %get-tuple-element.24.refs_1_.refs_2_.refs_5_), channel_id=1, source_target_pairs={{0,4},{2,6},{4,0},{6,2},{8,12},{10,14},{12,8},{14,10},{1,5},{3,7},... | collective-permute-start | bytes 233480 | tf_op jit(solution)/shard_map/ppermute | solution.py:29
  8.0 0.0 collective-permute-done.13
  8.0 1.9 %collective-permute-start.14 = (f32[96,128]{1,0:T(8,128)S(1)}, f32[96,128]{1,0:T(8,128)S(1)}, u32[]{:S(2)}, u32[]{:S(2)}) collective-permute-start(f32[96,128]{1,0:T(8,128)S(1)} %pad_maximum_fusion.3), channel_id=1, source_target_pairs={{0,16},{16,0},{1,17},{17,1},{2,18},{18,2},{3,19},{19,3},{4,20},{20... | collective-permute-start | bytes 147464 | tf_op jit(solution)/shard_map/ppermute | solution.py:29
  9.8 2.2 %collective-permute-done.refs_3_.refs_6_ = bf16[304,128]{1,0:T(8,128)(2,1)S(1)} collective-permute-done((bf16[304,128]{1,0:T(8,128)(2,1)S(1)}, bf16[304,128]{1,0:T(8,128)(2,1)S(1)}, u32[]{:S(2)}, u32[]{:S(2)}) %collective-permute-start) | collective-permute-done | bytes 77856 | tf_op jit(solution)/shard_map/ppermute | solution.py:29
  12.0 0.0 collective-permute-done.2.refs_4_.refs_7_
  12.0 1.6 %collective-permute-start.3 = (bf16[608,128]{1,0:T(8,128)(2,1)S(1)}, bf16[608,128]{1,0:T(8,128)(2,1)S(1)}, u32[]{:S(2)}, u32[]{:S(2)}) collective-permute-start(bf16[608,128]{1,0:T(8,128)(2,1)S(1)} %pad_maximum_fusion.1), channel_id=1, source_target_pairs={{0,2},{2,0},{4,6},{6,4},{8,10},{10,8},{12,14},{14,12},{1,3},{3,1},... | collective-permute-start | bytes 466952 | tf_op jit(solution)/shard_map/ppermute | solution.py:29
  13.6 1.1 %collective-permute-start.1 = (bf16[304,128]{1,0:T(8,128)(2,1)S(1)}, bf16[304,128]{1,0:T(8,128)(2,1)S(1)}, u32[]{:S(2)}, u32[]{:S(2)}) collective-permute-start(bf16[304,128]{1,0:T(8,128)(2,1)S(1)} %collective-permute-done.refs_3_.refs_6_), channel_id=1, source_target_pairs={{0,4},{2,6},{4,0},{6,2},{8,12},{10,14},{12,8},{14,10},{1,5},{3,7},... | collective-permute-start | bytes 233480 | tf_op jit(solution)/shard_map/ppermute | solution.py:29
  14.8 0.0 collective-permute-done.14
  14.8 0.9 %collective-permute-start.15 = (f32[192,128]{1,0:T(8,128)S(1)}, f32[192,128]{1,0:T(8,128)S(1)}, u32[]{:S(2)}, u32[]{:S(2)}) collective-permute-start(f32[192,128]{1,0:T(8,128)S(1)} %pad_maximum_fusion.2), channel_id=1, source_target_pairs={{0,4},{2,6},{4,0},{6,2},{8,12},{10,14},{12,8},{14,10},{1,5},{3,7},... | collective-permute-start | bytes 294920 | tf_op jit(solution)/shard_map/ppermute | solution.py:29
  15.7 0.5 %collective-permute-start.4 = (bf16[304,128]{1,0:T(8,128)(2,1)S(1)}, bf16[304,128]{1,0:T(8,128)(2,1)S(1)}, u32[]{:S(2)}, u32[]{:S(2)}) collective-permute-start(bf16[304,128]{1,0:T(8,128)(2,1)S(1)} %get-tuple-element.24.refs_1_.refs_2_.refs_5_), channel_id=1, source_target_pairs={{0,2},{2,0},{4,6},{6,4},{8,10},{10,8},{12,14},{14,12},{1,3},{3,1},... | collective-permute-start | bytes 233480 | tf_op jit(solution)/shard_map/ppermute | solution.py:29
  16.2 1.8 %collective-permute-done.1.refs_2_.refs_8_ = bf16[304,128]{1,0:T(8,128)(2,1)S(1)} collective-permute-done((bf16[304,128]{1,0:T(8,128)(2,1)S(1)}, bf16[304,128]{1,0:T(8,128)(2,1)S(1)}, u32[]{:S(2)}, u32[]{:S(2)}) %collective-permute-start.1) | collective-permute-done | bytes 77856 | tf_op jit(solution)/shard_map/ppermute | solution.py:29
  18.0 0.5 %collective-permute-start.5 = (bf16[304,128]{1,0:T(8,128)(2,1)S(1)}, bf16[304,128]{1,0:T(8,128)(2,1)S(1)}, u32[]{:S(2)}, u32[]{:S(2)}) collective-permute-start(bf16[304,128]{1,0:T(8,128)(2,1)S(1)} %collective-permute-done.1.refs_2_.refs_8_), channel_id=1, source_target_pairs={{0,2},{2,0},{4,6},{6,4},{8,10},{10,8},{12,14},{14,12},{1,3},{3,1},... | collective-permute-start | bytes 233480 | tf_op jit(solution)/shard_map/ppermute | solution.py:29
  18.5 1.6 %collective-permute-done.4.refs_5_.refs_9_ = bf16[304,128]{1,0:T(8,128)(2,1)S(1)} collective-permute-done((bf16[304,128]{1,0:T(8,128)(2,1)S(1)}, bf16[304,128]{1,0:T(8,128)(2,1)S(1)}, u32[]{:S(2)}, u32[]{:S(2)}) %collective-permute-start.4) | collective-permute-done | bytes 77856 | tf_op jit(solution)/shard_map/ppermute | solution.py:29
  20.1 1.7 %shard_map.130 = (f32[2048,128]{1,0:T(8,128)S(1)}, f32[2048,128]{1,0:T(8,128)S(1)}, f32[2048,128]{1,0:T(8,128)S(1)}) custom-call(bf16[128,2048]{1,0:T(8,128)(2,1)S(1)} %get-tuple-element.23.refs_0_.q, bf16[304,128]{1,0:T(8,128)(2,1)S(1)} %get-tuple-element.24.refs_1_.refs_2_.refs_5_, bf16[304,128]{1,0:T(8,128)(2,1)S(1)} %get-tuple-element.24.refs_1_.refs_2_.refs_5_, ...), custom_call_target="tpu_custom_call" | custom-call | tf_op jit(solution)/shard_map/pallas_call | solution.py:334
  21.8 0.0 collective-permute-done.3.refs_3_.refs_10_
  21.8 0.0 copy-start
  21.9 1.3 %shard_map.131 = (f32[2048,128]{1,0:T(8,128)S(1)}, f32[2048,128]{1,0:T(8,128)S(1)}, f32[2048,128]{1,0:T(8,128)S(1)}) custom-call(bf16[128,2048]{1,0:T(8,128)(2,1)S(1)} %get-tuple-element.23.refs_0_.q, bf16[304,128]{1,0:T(8,128)(2,1)S(1)} %get-tuple-element.24.refs_1_.refs_2_.refs_5_, bf16[304,128]{1,0:T(8,128)(2,1)S(1)} %collective-permute-done.1.refs_2_.refs_8_, ...), custom_call_target="tpu_custom_call" | custom-call | tf_op jit(solution)/shard_map/pallas_call | solution.py:334
  23.2 0.0 collective-permute-done.5.refs_11_
  23.2 0.0 copy-done
  23.2 2.6 %shard_map.132 = (f32[2048,128]{1,0:T(8,128)S(1)}, f32[2048,128]{1,0:T(8,128)S(1)}, f32[2048,128]{1,0:T(8,128)S(1)}, bf16[128,256]{1,0:T(8,128)(2,1)S(1)}) custom-call(bf16[128,2048]{1,0:T(8,128)(2,1)S(1)} %get-tuple-element.23.refs_0_.q, bf16[128,2048]{1,0:T(8,128)(2,1)S(1)} %bitcast.2, f32[2048,128]{1,0:T(8,128)S(1)} %get-tuple-element.28.refs_2_, ...), custom_call_target="tpu_custom_call" | custom-call | tf_op jit(solution)/shard_map/pallas_call | solution.py:345
  25.8 3.8 %collective-permute-start.6 = (bf16[128,256]{1,0:T(8,128)(2,1)S(1)}, bf16[128,256]{1,0:T(8,128)(2,1)S(1)}, u32[]{:S(2)}, u32[]{:S(2)}) collective-permute-start(bf16[128,256]{1,0:T(8,128)(2,1)S(1)} %get-tuple-element.34), channel_id=1, source_target_pairs={{0,12},{2,14},{4,8},{6,10},{8,4},{10,6},{12,0},{14,2},{16,28},{18,... | collective-permute-start | bytes 196616 | tf_op jit(solution)/shard_map/ppermute | solution.py:29
  29.5 0.0 collective-permute-start.7
  29.5 0.7 %collective-permute-start.8 = (bf16[128,256]{1,0:T(8,128)(2,1)S(1)}, bf16[128,256]{1,0:T(8,128)(2,1)S(1)}, u32[]{:S(2)}, u32[]{:S(2)}) collective-permute-start(bf16[128,256]{1,0:T(8,128)(2,1)S(1)} %get-tuple-element.34), channel_id=1, source_target_pairs={{0,4},{2,6},{4,0},{6,2},{8,12},{10,14},{12,8},{14,10},{16,20},{18,... | collective-permute-start | bytes 196616 | tf_op jit(solution)/shard_map/ppermute | solution.py:29
  30.2 0.0 collective-permute-done.15
  30.3 1.0 %collective-permute-start.16 = (f32[384,128]{1,0:T(8,128)S(1)}, f32[384,128]{1,0:T(8,128)S(1)}, u32[]{:S(2)}, u32[]{:S(2)}) collective-permute-start(f32[384,128]{1,0:T(8,128)S(1)} %pad_maximum_fusion.st_near), channel_id=1, source_target_pairs={{0,2},{2,0},{4,6},{6,4},{8,10},{10,8},{12,14},{14,12},{1,3},{3,1},... | collective-permute-start | bytes 589832 | tf_op jit(solution)/shard_map/ppermute | solution.py:29
  31.3 0.7 %collective-permute-done.6 = bf16[128,256]{1,0:T(8,128)(2,1)S(1)} collective-permute-done((bf16[128,256]{1,0:T(8,128)(2,1)S(1)}, bf16[128,256]{1,0:T(8,128)(2,1)S(1)}, u32[]{:S(2)}, u32[]{:S(2)}) %collective-permute-start.6) | collective-permute-done | bytes 65568 | tf_op jit(solution)/shard_map/ppermute | solution.py:29
  32.0 2.7 %collective-permute-done.7 = bf16[128,256]{1,0:T(8,128)(2,1)S(1)} collective-permute-done((bf16[128,256]{1,0:T(8,128)(2,1)S(1)}, bf16[128,256]{1,0:T(8,128)(2,1)S(1)}, u32[]{:S(2)}, u32[]{:S(2)}) %collective-permute-start.7) | collective-permute-done | bytes 65568 | tf_op jit(solution)/shard_map/ppermute | solution.py:29
  34.7 0.0 collective-permute-done.8
  34.8 1.6 %collective-permute-start.10 = (bf16[128,256]{1,0:T(8,128)(2,1)S(1)}, bf16[128,256]{1,0:T(8,128)(2,1)S(1)}, u32[]{:S(2)}, u32[]{:S(2)}) collective-permute-start(bf16[128,256]{1,0:T(8,128)(2,1)S(1)} %add_convert_fusion.refs_0_), channel_id=1, source_target_pairs={{0,16},{2,18},{4,20},{6,22},{8,24},{10,26},{12,28},{14,30},{16,0},... | collective-permute-start | bytes 196616 | tf_op jit(solution)/shard_map/ppermute | solution.py:29
  36.3 1.0 %collective-permute-start.11 = (bf16[128,256]{1,0:T(8,128)(2,1)S(1)}, bf16[128,256]{1,0:T(8,128)(2,1)S(1)}, u32[]{:S(2)}, u32[]{:S(2)}) collective-permute-start(bf16[128,256]{1,0:T(8,128)(2,1)S(1)} %add_convert_fusion.refs_0_), channel_id=1, source_target_pairs={{0,18},{2,16},{4,22},{6,20},{8,26},{10,24},{12,30},{14,28},{16,2},... | collective-permute-start | bytes 196616 | tf_op jit(solution)/shard_map/ppermute | solution.py:29
  37.3 1.0 %collective-permute-start.9 = (bf16[128,256]{1,0:T(8,128)(2,1)S(1)}, bf16[128,256]{1,0:T(8,128)(2,1)S(1)}, u32[]{:S(2)}, u32[]{:S(2)}) collective-permute-start(bf16[128,256]{1,0:T(8,128)(2,1)S(1)} %add_convert_fusion.refs_0_), channel_id=1, source_target_pairs={{0,2},{2,0},{4,6},{6,4},{8,10},{10,8},{12,14},{14,12},{16,18},{18,... | collective-permute-start | bytes 196616 | tf_op jit(solution)/shard_map/ppermute | solution.py:29
  38.3 0.8 %collective-permute-done.10.refs_2_ = bf16[128,256]{1,0:T(8,128)(2,1)S(1)} collective-permute-done((bf16[128,256]{1,0:T(8,128)(2,1)S(1)}, bf16[128,256]{1,0:T(8,128)(2,1)S(1)}, u32[]{:S(2)}, u32[]{:S(2)}) %collective-permute-start.10) | collective-permute-done | bytes 65568 | tf_op jit(solution)/shard_map/ppermute | solution.py:29
  39.1 2.4 %collective-permute-done.11.refs_3_ = bf16[128,256]{1,0:T(8,128)(2,1)S(1)} collective-permute-done((bf16[128,256]{1,0:T(8,128)(2,1)S(1)}, bf16[128,256]{1,0:T(8,128)(2,1)S(1)}, u32[]{:S(2)}, u32[]{:S(2)}) %collective-permute-start.11) | collective-permute-done | bytes 65568 | tf_op jit(solution)/shard_map/ppermute | solution.py:29
  41.5 0.6 %collective-permute-done.9.refs_1_ = bf16[128,256]{1,0:T(8,128)(2,1)S(1)} collective-permute-done((bf16[128,256]{1,0:T(8,128)(2,1)S(1)}, bf16[128,256]{1,0:T(8,128)(2,1)S(1)}, u32[]{:S(2)}, u32[]{:S(2)}) %collective-permute-start.9) | collective-permute-done | bytes 65568 | tf_op jit(solution)/shard_map/ppermute | solution.py:29
  42.2 0.2 shard_map.133
  42.4 0.1 collective-permute-start.12
  42.5 1.2 %collective-permute-done.12.sq_b = f32[8,128]{1,0:T(8,128)S(1)} collective-permute-done((f32[8,128]{1,0:T(8,128)S(1)}, f32[8,128]{1,0:T(8,128)S(1)}, u32[]{:S(2)}, u32[]{:S(2)}) %collective-permute-start.12) | collective-permute-done | bytes 4128 | tf_op jit(solution)/shard_map/ppermute | solution.py:29
  43.6 0.0 collective-permute-done.16.st_far
  43.6 2.0 %shard_map.134 = (bf16[128,2048]{1,0:T(8,128)(2,1)}, f32[16,1,128]{2,1,0:T(1,128)}, f32[16,1,128]{2,1,0:T(1,128)}, f32[16,1,128]{2,1,0:T(1,128)}) custom-call(bf16[128,2048]{1,0:T(8,128)(2,1)S(1)} %get-tuple-element.23.refs_0_.q, f32[2048,128]{1,0:T(8,128)S(1)} %get-tuple-element.31.acc_in, f32[2048,128]{1,0:T(8,128)S(1)} %get-tuple-element.32.total_in, ...), custom_call_target="tpu_custom_call" | custom-call | tf_op jit(solution)/shard_map/pallas_call | solution.py:361
  (5 shorter events, 0.1 us)
Async XLA Ops:
  1.9 6.0 %collective-permute-start.13 = (f32[48,128]{1,0:T(8,128)S(1)}, f32[48,128]{1,0:T(8,128)S(1)}, u32[]{:S(2)}, u32[]{:S(2)}) collective-permute-start(f32[48,128]{1,0:T(8,128)S(1)} %get-tuple-element.37), channel_id=1, source_target_pairs={{0,8},{2,10},{4,12},{6,14},{8,0},{10,2},{12,4},{14,6},{1,9},{3,11}... | collective-permute-start | bytes 73736 | tf_op jit(solution)/shard_map/ppermute | solution.py:29
  6.0 6.0 %collective-permute-start = (bf16[304,128]{1,0:T(8,128)(2,1)S(1)}, bf16[304,128]{1,0:T(8,128)(2,1)S(1)}, u32[]{:S(2)}, u32[]{:S(2)}) collective-permute-start(bf16[304,128]{1,0:T(8,128)(2,1)S(1)} %get-tuple-element.24.refs_1_.refs_2_.refs_5_), channel_id=1, source_target_pairs={{0,8},{2,10},{4,12},{6,14},{8,0},{10,2},{12,4},{14,6},{1,9},{3,11}... | collective-permute-start | bytes 233480 | tf_op jit(solution)/shard_map/ppermute | solution.py:29
  6.1 5.9 %collective-permute-start.2 = (bf16[304,128]{1,0:T(8,128)(2,1)S(1)}, bf16[304,128]{1,0:T(8,128)(2,1)S(1)}, u32[]{:S(2)}, u32[]{:S(2)}) collective-permute-start(bf16[304,128]{1,0:T(8,128)(2,1)S(1)} %get-tuple-element.24.refs_1_.refs_2_.refs_5_), channel_id=1, source_target_pairs={{0,4},{2,6},{4,0},{6,2},{8,12},{10,14},{12,8},{14,10},{1,5},{3,7},... | collective-permute-start | bytes 233480 | tf_op jit(solution)/shard_map/ppermute | solution.py:29
  8.0 6.8 %collective-permute-start.14 = (f32[96,128]{1,0:T(8,128)S(1)}, f32[96,128]{1,0:T(8,128)S(1)}, u32[]{:S(2)}, u32[]{:S(2)}) collective-permute-start(f32[96,128]{1,0:T(8,128)S(1)} %pad_maximum_fusion.3), channel_id=1, source_target_pairs={{0,16},{16,0},{1,17},{17,1},{2,18},{18,2},{3,19},{19,3},{4,20},{20... | collective-permute-start | bytes 147464 | tf_op jit(solution)/shard_map/ppermute | solution.py:29
  12.0 9.8 %collective-permute-start.3 = (bf16[608,128]{1,0:T(8,128)(2,1)S(1)}, bf16[608,128]{1,0:T(8,128)(2,1)S(1)}, u32[]{:S(2)}, u32[]{:S(2)}) collective-permute-start(bf16[608,128]{1,0:T(8,128)(2,1)S(1)} %pad_maximum_fusion.1), channel_id=1, source_target_pairs={{0,2},{2,0},{4,6},{6,4},{8,10},{10,8},{12,14},{14,12},{1,3},{3,1},... | collective-permute-start | bytes 466952 | tf_op jit(solution)/shard_map/ppermute | solution.py:29
  13.6 4.4 %collective-permute-start.1 = (bf16[304,128]{1,0:T(8,128)(2,1)S(1)}, bf16[304,128]{1,0:T(8,128)(2,1)S(1)}, u32[]{:S(2)}, u32[]{:S(2)}) collective-permute-start(bf16[304,128]{1,0:T(8,128)(2,1)S(1)} %collective-permute-done.refs_3_.refs_6_), channel_id=1, source_target_pairs={{0,4},{2,6},{4,0},{6,2},{8,12},{10,14},{12,8},{14,10},{1,5},{3,7},... | collective-permute-start | bytes 233480 | tf_op jit(solution)/shard_map/ppermute | solution.py:29
  14.8 15.5 %collective-permute-start.15 = (f32[192,128]{1,0:T(8,128)S(1)}, f32[192,128]{1,0:T(8,128)S(1)}, u32[]{:S(2)}, u32[]{:S(2)}) collective-permute-start(f32[192,128]{1,0:T(8,128)S(1)} %pad_maximum_fusion.2), channel_id=1, source_target_pairs={{0,4},{2,6},{4,0},{6,2},{8,12},{10,14},{12,8},{14,10},{1,5},{3,7},... | collective-permute-start | bytes 294920 | tf_op jit(solution)/shard_map/ppermute | solution.py:29
  15.7 4.4 %collective-permute-start.4 = (bf16[304,128]{1,0:T(8,128)(2,1)S(1)}, bf16[304,128]{1,0:T(8,128)(2,1)S(1)}, u32[]{:S(2)}, u32[]{:S(2)}) collective-permute-start(bf16[304,128]{1,0:T(8,128)(2,1)S(1)} %get-tuple-element.24.refs_1_.refs_2_.refs_5_), channel_id=1, source_target_pairs={{0,2},{2,0},{4,6},{6,4},{8,10},{10,8},{12,14},{14,12},{1,3},{3,1},... | collective-permute-start | bytes 233480 | tf_op jit(solution)/shard_map/ppermute | solution.py:29
  18.0 5.2 %collective-permute-start.5 = (bf16[304,128]{1,0:T(8,128)(2,1)S(1)}, bf16[304,128]{1,0:T(8,128)(2,1)S(1)}, u32[]{:S(2)}, u32[]{:S(2)}) collective-permute-start(bf16[304,128]{1,0:T(8,128)(2,1)S(1)} %collective-permute-done.1.refs_2_.refs_8_), channel_id=1, source_target_pairs={{0,2},{2,0},{4,6},{6,4},{8,10},{10,8},{12,14},{14,12},{1,3},{3,1},... | collective-permute-start | bytes 233480 | tf_op jit(solution)/shard_map/ppermute | solution.py:29
  21.8 1.4 %copy-start = (bf16[1,128,2048]{2,1,0:T(8,128)(2,1)S(1)}, bf16[1,128,2048]{2,1,0:T(8,128)(2,1)}, u32[]{:S(2)}) copy-start(bf16[1,128,2048]{2,1,0:T(8,128)(2,1)} %param.11) | copy-start | bytes 1572868
  25.8 6.2 %collective-permute-start.6 = (bf16[128,256]{1,0:T(8,128)(2,1)S(1)}, bf16[128,256]{1,0:T(8,128)(2,1)S(1)}, u32[]{:S(2)}, u32[]{:S(2)}) collective-permute-start(bf16[128,256]{1,0:T(8,128)(2,1)S(1)} %get-tuple-element.34), channel_id=1, source_target_pairs={{0,12},{2,14},{4,8},{6,10},{8,4},{10,6},{12,0},{14,2},{16,28},{18,... | collective-permute-start | bytes 196616 | tf_op jit(solution)/shard_map/ppermute | solution.py:29
  29.5 5.2 %collective-permute-start.7 = (bf16[128,256]{1,0:T(8,128)(2,1)S(1)}, bf16[128,256]{1,0:T(8,128)(2,1)S(1)}, u32[]{:S(2)}, u32[]{:S(2)}) collective-permute-start(bf16[128,256]{1,0:T(8,128)(2,1)S(1)} %get-tuple-element.34), channel_id=1, source_target_pairs={{0,8},{2,10},{4,12},{6,14},{8,0},{10,2},{12,4},{14,6},{16,24},{18,... | collective-permute-start | bytes 196616 | tf_op jit(solution)/shard_map/ppermute | solution.py:29
  29.5 5.2 %collective-permute-start.8 = (bf16[128,256]{1,0:T(8,128)(2,1)S(1)}, bf16[128,256]{1,0:T(8,128)(2,1)S(1)}, u32[]{:S(2)}, u32[]{:S(2)}) collective-permute-start(bf16[128,256]{1,0:T(8,128)(2,1)S(1)} %get-tuple-element.34), channel_id=1, source_target_pairs={{0,4},{2,6},{4,0},{6,2},{8,12},{10,14},{12,8},{14,10},{16,20},{18,... | collective-permute-start | bytes 196616 | tf_op jit(solution)/shard_map/ppermute | solution.py:29
  30.3 13.3 %collective-permute-start.16 = (f32[384,128]{1,0:T(8,128)S(1)}, f32[384,128]{1,0:T(8,128)S(1)}, u32[]{:S(2)}, u32[]{:S(2)}) collective-permute-start(f32[384,128]{1,0:T(8,128)S(1)} %pad_maximum_fusion.st_near), channel_id=1, source_target_pairs={{0,2},{2,0},{4,6},{6,4},{8,10},{10,8},{12,14},{14,12},{1,3},{3,1},... | collective-permute-start | bytes 589832 | tf_op jit(solution)/shard_map/ppermute | solution.py:29
  34.8 4.3 %collective-permute-start.10 = (bf16[128,256]{1,0:T(8,128)(2,1)S(1)}, bf16[128,256]{1,0:T(8,128)(2,1)S(1)}, u32[]{:S(2)}, u32[]{:S(2)}) collective-permute-start(bf16[128,256]{1,0:T(8,128)(2,1)S(1)} %add_convert_fusion.refs_0_), channel_id=1, source_target_pairs={{0,16},{2,18},{4,20},{6,22},{8,24},{10,26},{12,28},{14,30},{16,0},... | collective-permute-start | bytes 196616 | tf_op jit(solution)/shard_map/ppermute | solution.py:29
  36.3 5.2 %collective-permute-start.11 = (bf16[128,256]{1,0:T(8,128)(2,1)S(1)}, bf16[128,256]{1,0:T(8,128)(2,1)S(1)}, u32[]{:S(2)}, u32[]{:S(2)}) collective-permute-start(bf16[128,256]{1,0:T(8,128)(2,1)S(1)} %add_convert_fusion.refs_0_), channel_id=1, source_target_pairs={{0,18},{2,16},{4,22},{6,20},{8,26},{10,24},{12,30},{14,28},{16,2},... | collective-permute-start | bytes 196616 | tf_op jit(solution)/shard_map/ppermute | solution.py:29
  37.3 4.9 %collective-permute-start.9 = (bf16[128,256]{1,0:T(8,128)(2,1)S(1)}, bf16[128,256]{1,0:T(8,128)(2,1)S(1)}, u32[]{:S(2)}, u32[]{:S(2)}) collective-permute-start(bf16[128,256]{1,0:T(8,128)(2,1)S(1)} %add_convert_fusion.refs_0_), channel_id=1, source_target_pairs={{0,2},{2,0},{4,6},{6,4},{8,10},{10,8},{12,14},{14,12},{16,18},{18,... | collective-permute-start | bytes 196616 | tf_op jit(solution)/shard_map/ppermute | solution.py:29
  42.4 1.2 %collective-permute-start.12 = (f32[8,128]{1,0:T(8,128)S(1)}, f32[8,128]{1,0:T(8,128)S(1)}, u32[]{:S(2)}, u32[]{:S(2)}) collective-permute-start(f32[8,128]{1,0:T(8,128)S(1)} %get-tuple-element.36.sq_a), channel_id=1, source_target_pairs={{0,1},{1,0},{2,3},{3,2},{4,5},{5,4},{6,7},{7,6},{8,9},{9,8},{10,11... | collective-permute-start | bytes 12296 | tf_op jit(solution)/shard_map/ppermute | solution.py:29

commit v2 on v1

--- a/solution.py
+++ b/solution.py
@@ -53,7 +53,7 @@
     return jnp.dot(a, b, preferred_element_type=f32)
 
 
-def pack_kernel(k, v, pos, ck, cv, ma, m1, m2, q, msg, st, q_here, line, sems):
+def pack_kernel(k, v, pos, ck, cv, ma, m1, m2, msg, st, line, sems):
     rows, crows, hd = k.shape[1], ck.shape[0], k.shape[2]
     at = 2 * rows
     copies = [
@@ -64,7 +64,6 @@
         (pos, line),
     ]
     copies += [(ref.at[:, 0, :], st.at[n * crows : (n + 1) * crows]) for n, ref in enumerate((ma, m1, m2))]
-    copies.append((q.at[0], q_here))
     started = [pltpu.make_async_copy(x, y, sems.at[n]) for n, (x, y) in enumerate(copies)]
     for copy in started:
         copy.start()
@@ -77,6 +76,12 @@
     row = lax.broadcasted_iota(jnp.int32, (16, hd), 0)
     both = jnp.where(row == 0, jnp.broadcast_to(hi, (16, hd)), jnp.broadcast_to(lo, (16, hd)))
     msg[at : at + 16] = both.astype(bf16)
+
+
+def fetch_kernel(source, target, sem):
+    copy = pltpu.make_async_copy(source, target, sem)
+    copy.start()
+    copy.wait()
 
 
 def split(refs, stride):
@@ -299,20 +304,20 @@
     masks = [0]
     for s in steps:
         masks += [m ^ s for m in masks]
-    msg, st, q = pl.pallas_call(
+    msg, st = pl.pallas_call(
         pack_kernel,
-        out_shape=(sds((stride, hd), bf16), sds((3 * crows, master.shape[2]), f32), sds(queries.shape[1:], queries.dtype)),
-        in_specs=[pl.BlockSpec(memory_space=pltpu.HBM)] * 9,
-        out_specs=(VMEM, VMEM, VMEM),
-        scratch_shapes=[pltpu.VMEM(doc_pos.shape, jnp.int32), pltpu.SemaphoreType.DMA((9,))],
+        out_shape=(sds((stride, hd), bf16), sds((3 * crows, master.shape[2]), f32)),
+        in_specs=[pl.BlockSpec(memory_space=pltpu.HBM)] * 8,
+        out_specs=(VMEM, VMEM),
+        scratch_shapes=[pltpu.VMEM(doc_pos.shape, jnp.int32), pltpu.SemaphoreType.DMA((8,))],
         compiler_params=pltpu.CompilerParams(vmem_limit_bytes=8 * 2**20),
     )(
         *(
             pltpu.with_memory_space_constraint(x, pltpu.HBM)
-            for x in (document_keys, document_values, doc_pos, cart_keys, cartridge_values, master, first_moment1, second_moment2, queries)
+            for x in (document_keys, document_values, doc_pos, cart_keys, cartridge_values, master, first_moment1, second_moment2)
         )
     )
-    t = targets[0]
+    q, t = queries[0], targets[0]
     cart = n_ctx * crows
     shapes = (sds((rows * group, hd), f32),) * 3
     last = steps[-1]
@@ -328,9 +333,17 @@
     msgs = held + mirrored
     tail = mirrored[-1].shape[0] // stride
     left = max(2, tail)
+    q = pl.pallas_call(
+        fetch_kernel,
+        out_shape=sds(q.shape, q.dtype),
+        in_specs=[pl.BlockSpec(memory_space=pltpu.HBM)],
+        out_specs=VMEM,
+        scratch_shapes=[pltpu.SemaphoreType.DMA],
+        compiler_params=pltpu.CompilerParams(vmem_limit_bytes=8 * 2**20),
+    )(pltpu.with_memory_space_constraint(q, pltpu.HBM))
 
     def document(some, skipped, state):
-        body = functools.partial(chunk_kernel, skipped, len(some), scale, math.gcd(group, 2), rows, stride)
+        body = functools.partial(chunk_kernel, skipped, len(some), scale, math.gcd(group, 4 if state else 2), rows, stride)
         return call(body, shapes, 2 + len(some) + len(state))(q, msg, *some, *state)
 
     state = document(held[:-1] + mirrored[:-2], 0, ())

time: 45.8 us -> 45.4 us (level)
  waiting for transfers between devices: 14 us -> 13 us
  Pallas kernels: 9.06 us -> 9.67 us
    ppermute x17, waiting for transfers between devices: 14 us -> 13 us  [swap(): return lax.ppermute(x, axis, [(i, i ^ mask) for i in range(size)])]
    pallas_call x0 -> x1, Pallas kernels: none -> 1.05 us  [local(): pl.pallas_call(fetch_kernel, out_shape=sds(q.shape, q.dtype), in_specs=[p...]
  transfers between devices with their start and end apart: 17 -> 17, of which waited for: 9 -> 9; matrix products, arithmetic and copies ran while one was open for 0% -> 0% of each run, Pallas kernels for 13% -> 15%
where the time goes in v2:
time: 45.4 us; the launch traced here: 45.2 us
  starting transfers between devices  21.7 us (48%)
  waiting for transfers between devices  13 us (29%)
  Pallas kernels  9.67 us (21%)
  between operations  0.75 us (2%)
    ppermute x17, starting transfers between devices, swap(): return lax.ppermute(x, axis, [(i, i ^ mask) for i in range(size)])  21.7 us
    ppermute x17, waiting for transfers between devices, swap(): return lax.ppermute(x, axis, [(i, i ^ mask) for i in range(size)])  13 us
    pallas_call x2, Pallas kernels, document(): return call(body, shapes, 2 + len(some) + len(state))(q, msg, *some, *state)  2.97 us
    pallas_call x1, Pallas kernels, local(): call(body, shapes + (sds((cart, 2 * hd), bf16),), 5 + len(msgs))  2.57 us
    pallas_call x1, Pallas kernels, local(): call(functools.partial(final_kernel, masks, chain, n_dp, scale, math.gcd(...  2 us
    pallas_call x1, Pallas kernels, local(): pl.pallas_call(fetch_kernel, out_shape=sds(q.shape, q.dtype), in_specs=[p...  1.05 us
  transfers between devices with their start and end apart: 17, of which 9 were waited for; matrix products, arithmetic and copies ran while one was open for 0% of the time, Pallas kernels for 15%

profile of v2, /device:TPU:0, one launch (start us, length us, event | category | flops | bytes accessed | tf_op | source)
XLA Modules:
  0.0 45.2 jit_solution(13128954182001811916)
XLA Ops:
  0.6 0.9 %shard_map.130 = (bf16[304,128]{1,0:T(8,128)(2,1)S(1)}, f32[48,128]{1,0:T(8,128)S(1)}) custom-call(bf16[1,128,128]{2,1,0:T(8,128)(2,1)} %k.1, bf16[1,128,128]{2,1,0:T(8,128)(2,1)} %v.1, s32[1,128]{1,0:T(1,128)} %pos.1, bf16[16,128]{1,0:T(8,128)(2,1)} %ck.1, bf16[16,128]{1,0:T(8,128)(2,1)} %cv.1, f32[16,1,128]{2,1,0:T(1,128)} %ma.1, f32[16,1,128]{2,1,0:T(1,128)} %m1.1, ...), custom_call_target="tpu_custom_call" | custom-call | tf_op jit(solution)/shard_map/pallas_call | solution.py:307
  1.5 4.1 %collective-permute-start.13 = (f32[48,128]{1,0:T(8,128)S(1)}, f32[48,128]{1,0:T(8,128)S(1)}, u32[]{:S(2)}, u32[]{:S(2)}) collective-permute-start(f32[48,128]{1,0:T(8,128)S(1)} %get-tuple-element.35), channel_id=1, source_target_pairs={{0,8},{2,10},{4,12},{6,14},{8,0},{10,2},{12,4},{14,6},{1,9},{3,11}... | collective-permute-start | bytes 73736 | tf_op jit(solution)/shard_map/ppermute | solution.py:29
  5.7 0.1 collective-permute-start
  5.7 1.8 %collective-permute-start.2 = (bf16[304,128]{1,0:T(8,128)(2,1)S(1)}, bf16[304,128]{1,0:T(8,128)(2,1)S(1)}, u32[]{:S(2)}, u32[]{:S(2)}) collective-permute-start(bf16[304,128]{1,0:T(8,128)(2,1)S(1)} %get-tuple-element.22.refs_1_.refs_2_.refs_5_), channel_id=1, source_target_pairs={{0,4},{2,6},{4,0},{6,2},{8,12},{10,14},{12,8},{14,10},{1,5},{3,7},... | collective-permute-start | bytes 233480 | tf_op jit(solution)/shard_map/ppermute | solution.py:29
  7.6 0.0 collective-permute-done.13
  7.6 1.9 %collective-permute-start.14 = (f32[96,128]{1,0:T(8,128)S(1)}, f32[96,128]{1,0:T(8,128)S(1)}, u32[]{:S(2)}, u32[]{:S(2)}) collective-permute-start(f32[96,128]{1,0:T(8,128)S(1)} %pad_maximum_fusion.3), channel_id=1, source_target_pairs={{0,16},{16,0},{1,17},{17,1},{2,18},{18,2},{3,19},{19,3},{4,20},{20... | collective-permute-start | bytes 147464 | tf_op jit(solution)/shard_map/ppermute | solution.py:29
  9.4 2.2 %collective-permute-done.refs_3_.refs_6_ = bf16[304,128]{1,0:T(8,128)(2,1)S(1)} collective-permute-done((bf16[304,128]{1,0:T(8,128)(2,1)S(1)}, bf16[304,128]{1,0:T(8,128)(2,1)S(1)}, u32[]{:S(2)}, u32[]{:S(2)}) %collective-permute-start) | collective-permute-done | bytes 77856 | tf_op jit(solution)/shard_map/ppermute | solution.py:29
  11.6 0.0 collective-permute-done.2.refs_4_.refs_7_
  11.7 1.6 %collective-permute-start.3 = (bf16[608,128]{1,0:T(8,128)(2,1)S(1)}, bf16[608,128]{1,0:T(8,128)(2,1)S(1)}, u32[]{:S(2)}, u32[]{:S(2)}) collective-permute-start(bf16[608,128]{1,0:T(8,128)(2,1)S(1)} %pad_maximum_fusion.1), channel_id=1, source_target_pairs={{0,2},{2,0},{4,6},{6,4},{8,10},{10,8},{12,14},{14,12},{1,3},{3,1},... | collective-permute-start | bytes 466952 | tf_op jit(solution)/shard_map/ppermute | solution.py:29
  13.2 1.1 %collective-permute-start.1 = (bf16[304,128]{1,0:T(8,128)(2,1)S(1)}, bf16[304,128]{1,0:T(8,128)(2,1)S(1)}, u32[]{:S(2)}, u32[]{:S(2)}) collective-permute-start(bf16[304,128]{1,0:T(8,128)(2,1)S(1)} %collective-permute-done.refs_3_.refs_6_), channel_id=1, source_target_pairs={{0,4},{2,6},{4,0},{6,2},{8,12},{10,14},{12,8},{14,10},{1,5},{3,7},... | collective-permute-start | bytes 233480 | tf_op jit(solution)/shard_map/ppermute | solution.py:29
  14.4 0.0 collective-permute-done.14
  14.4 0.9 %collective-permute-start.15 = (f32[192,128]{1,0:T(8,128)S(1)}, f32[192,128]{1,0:T(8,128)S(1)}, u32[]{:S(2)}, u32[]{:S(2)}) collective-permute-start(f32[192,128]{1,0:T(8,128)S(1)} %pad_maximum_fusion.2), channel_id=1, source_target_pairs={{0,4},{2,6},{4,0},{6,2},{8,12},{10,14},{12,8},{14,10},{1,5},{3,7},... | collective-permute-start | bytes 294920 | tf_op jit(solution)/shard_map/ppermute | solution.py:29
  15.4 0.5 %collective-permute-start.4 = (bf16[304,128]{1,0:T(8,128)(2,1)S(1)}, bf16[304,128]{1,0:T(8,128)(2,1)S(1)}, u32[]{:S(2)}, u32[]{:S(2)}) collective-permute-start(bf16[304,128]{1,0:T(8,128)(2,1)S(1)} %get-tuple-element.22.refs_1_.refs_2_.refs_5_), channel_id=1, source_target_pairs={{0,2},{2,0},{4,6},{6,4},{8,10},{10,8},{12,14},{14,12},{1,3},{3,1},... | collective-permute-start | bytes 233480 | tf_op jit(solution)/shard_map/ppermute | solution.py:29
  15.9 1.8 %collective-permute-done.1.refs_2_.refs_8_ = bf16[304,128]{1,0:T(8,128)(2,1)S(1)} collective-permute-done((bf16[304,128]{1,0:T(8,128)(2,1)S(1)}, bf16[304,128]{1,0:T(8,128)(2,1)S(1)}, u32[]{:S(2)}, u32[]{:S(2)}) %collective-permute-start.1) | collective-permute-done | bytes 77856 | tf_op jit(solution)/shard_map/ppermute | solution.py:29
  17.6 0.5 %collective-permute-start.5 = (bf16[304,128]{1,0:T(8,128)(2,1)S(1)}, bf16[304,128]{1,0:T(8,128)(2,1)S(1)}, u32[]{:S(2)}, u32[]{:S(2)}) collective-permute-start(bf16[304,128]{1,0:T(8,128)(2,1)S(1)} %collective-permute-done.1.refs_2_.refs_8_), channel_id=1, source_target_pairs={{0,2},{2,0},{4,6},{6,4},{8,10},{10,8},{12,14},{14,12},{1,3},{3,1},... | collective-permute-start | bytes 233480 | tf_op jit(solution)/shard_map/ppermute | solution.py:29
  18.2 1.0 %shard_map.129.refs_0_.q = bf16[128,2048]{1,0:T(8,128)(2,1)S(1)} custom-call(bf16[128,2048]{1,0:T(8,128)(2,1)} %bitcast.4), custom_call_target="tpu_custom_call" | custom-call | tf_op jit(solution)/shard_map/pallas_call | solution.py:336
  19.2 0.5 %collective-permute-done.4.refs_5_.refs_9_ = bf16[304,128]{1,0:T(8,128)(2,1)S(1)} collective-permute-done((bf16[304,128]{1,0:T(8,128)(2,1)S(1)}, bf16[304,128]{1,0:T(8,128)(2,1)S(1)}, u32[]{:S(2)}, u32[]{:S(2)}) %collective-permute-start.4) | collective-permute-done | bytes 77856 | tf_op jit(solution)/shard_map/ppermute | solution.py:29
  19.8 1.7 %shard_map.131 = (f32[2048,128]{1,0:T(8,128)S(1)}, f32[2048,128]{1,0:T(8,128)S(1)}, f32[2048,128]{1,0:T(8,128)S(1)}) custom-call(bf16[128,2048]{1,0:T(8,128)(2,1)S(1)} %shard_map.129.refs_0_.q, bf16[304,128]{1,0:T(8,128)(2,1)S(1)} %get-tuple-element.22.refs_1_.refs_2_.refs_5_, bf16[304,128]{1,0:T(8,128)(2,1)S(1)} %get-tuple-element.22.refs_1_.refs_2_.refs_5_, ...), custom_call_target="tpu_custom_call" | custom-call | tf_op jit(solution)/shard_map/pallas_call | solution.py:347
  21.4 0.0 collective-permute-done.3.refs_3_.refs_10_
  21.5 0.0 copy-start
  21.5 1.3 %shard_map.132 = (f32[2048,128]{1,0:T(8,128)S(1)}, f32[2048,128]{1,0:T(8,128)S(1)}, f32[2048,128]{1,0:T(8,128)S(1)}) custom-call(bf16[128,2048]{1,0:T(8,128)(2,1)S(1)} %shard_map.129.refs_0_.q, bf16[304,128]{1,0:T(8,128)(2,1)S(1)} %get-tuple-element.22.refs_1_.refs_2_.refs_5_, bf16[304,128]{1,0:T(8,128)(2,1)S(1)} %collective-permute-done.1.refs_2_.refs_8_, ...), custom_call_target="tpu_custom_call" | custom-call | tf_op jit(solution)/shard_map/pallas_call | solution.py:347
  22.8 0.0 collective-permute-done.5.refs_11_
  22.8 0.0 copy-done
  22.8 2.6 %shard_map.133 = (f32[2048,128]{1,0:T(8,128)S(1)}, f32[2048,128]{1,0:T(8,128)S(1)}, f32[2048,128]{1,0:T(8,128)S(1)}, bf16[128,256]{1,0:T(8,128)(2,1)S(1)}) custom-call(bf16[128,2048]{1,0:T(8,128)(2,1)S(1)} %shard_map.129.refs_0_.q, bf16[128,2048]{1,0:T(8,128)(2,1)S(1)} %bitcast.3, f32[2048,128]{1,0:T(8,128)S(1)} %get-tuple-element.26.refs_2_, ...), custom_call_target="tpu_custom_call" | custom-call | tf_op jit(solution)/shard_map/pallas_call | solution.py:358
  25.4 3.7 %collective-permute-start.6 = (bf16[128,256]{1,0:T(8,128)(2,1)S(1)}, bf16[128,256]{1,0:T(8,128)(2,1)S(1)}, u32[]{:S(2)}, u32[]{:S(2)}) collective-permute-start(bf16[128,256]{1,0:T(8,128)(2,1)S(1)} %get-tuple-element.32), channel_id=1, source_target_pairs={{0,12},{2,14},{4,8},{6,10},{8,4},{10,6},{12,0},{14,2},{16,28},{18,... | collective-permute-start | bytes 196616 | tf_op jit(solution)/shard_map/ppermute | solution.py:29
  29.1 0.0 collective-permute-start.7
  29.1 0.7 %collective-permute-start.8 = (bf16[128,256]{1,0:T(8,128)(2,1)S(1)}, bf16[128,256]{1,0:T(8,128)(2,1)S(1)}, u32[]{:S(2)}, u32[]{:S(2)}) collective-permute-start(bf16[128,256]{1,0:T(8,128)(2,1)S(1)} %get-tuple-element.32), channel_id=1, source_target_pairs={{0,4},{2,6},{4,0},{6,2},{8,12},{10,14},{12,8},{14,10},{16,20},{18,... | collective-permute-start | bytes 196616 | tf_op jit(solution)/shard_map/ppermute | solution.py:29
  29.8 0.0 collective-permute-done.15
  29.8 1.1 %collective-permute-start.16 = (f32[384,128]{1,0:T(8,128)S(1)}, f32[384,128]{1,0:T(8,128)S(1)}, u32[]{:S(2)}, u32[]{:S(2)}) collective-permute-start(f32[384,128]{1,0:T(8,128)S(1)} %pad_maximum_fusion.st_near), channel_id=1, source_target_pairs={{0,2},{2,0},{4,6},{6,4},{8,10},{10,8},{12,14},{14,12},{1,3},{3,1},... | collective-permute-start | bytes 589832 | tf_op jit(solution)/shard_map/ppermute | solution.py:29
  30.9 0.7 %collective-permute-done.6 = bf16[128,256]{1,0:T(8,128)(2,1)S(1)} collective-permute-done((bf16[128,256]{1,0:T(8,128)(2,1)S(1)}, bf16[128,256]{1,0:T(8,128)(2,1)S(1)}, u32[]{:S(2)}, u32[]{:S(2)}) %collective-permute-start.6) | collective-permute-done | bytes 65568 | tf_op jit(solution)/shard_map/ppermute | solution.py:29
  31.6 2.7 %collective-permute-done.7 = bf16[128,256]{1,0:T(8,128)(2,1)S(1)} collective-permute-done((bf16[128,256]{1,0:T(8,128)(2,1)S(1)}, bf16[128,256]{1,0:T(8,128)(2,1)S(1)}, u32[]{:S(2)}, u32[]{:S(2)}) %collective-permute-start.7) | collective-permute-done | bytes 65568 | tf_op jit(solution)/shard_map/ppermute | solution.py:29
  34.3 0.0 collective-permute-done.8
  34.3 1.6 %collective-permute-start.10 = (bf16[128,256]{1,0:T(8,128)(2,1)S(1)}, bf16[128,256]{1,0:T(8,128)(2,1)S(1)}, u32[]{:S(2)}, u32[]{:S(2)}) collective-permute-start(bf16[128,256]{1,0:T(8,128)(2,1)S(1)} %add_convert_fusion.refs_0_), channel_id=1, source_target_pairs={{0,16},{2,18},{4,20},{6,22},{8,24},{10,26},{12,28},{14,30},{16,0},... | collective-permute-start | bytes 196616 | tf_op jit(solution)/shard_map/ppermute | solution.py:29
  35.9 1.0 %collective-permute-start.11 = (bf16[128,256]{1,0:T(8,128)(2,1)S(1)}, bf16[128,256]{1,0:T(8,128)(2,1)S(1)}, u32[]{:S(2)}, u32[]{:S(2)}) collective-permute-start(bf16[128,256]{1,0:T(8,128)(2,1)S(1)} %add_convert_fusion.refs_0_), channel_id=1, source_target_pairs={{0,18},{2,16},{4,22},{6,20},{8,26},{10,24},{12,30},{14,28},{16,2},... | collective-permute-start | bytes 196616 | tf_op jit(solution)/shard_map/ppermute | solution.py:29
  36.9 1.0 %collective-permute-start.9 = (bf16[128,256]{1,0:T(8,128)(2,1)S(1)}, bf16[128,256]{1,0:T(8,128)(2,1)S(1)}, u32[]{:S(2)}, u32[]{:S(2)}) collective-permute-start(bf16[128,256]{1,0:T(8,128)(2,1)S(1)} %add_convert_fusion.refs_0_), channel_id=1, source_target_pairs={{0,2},{2,0},{4,6},{6,4},{8,10},{10,8},{12,14},{14,12},{16,18},{18,... | collective-permute-start | bytes 196616 | tf_op jit(solution)/shard_map/ppermute | solution.py:29
  37.9 0.8 %collective-permute-done.10.refs_2_ = bf16[128,256]{1,0:T(8,128)(2,1)S(1)} collective-permute-done((bf16[128,256]{1,0:T(8,128)(2,1)S(1)}, bf16[128,256]{1,0:T(8,128)(2,1)S(1)}, u32[]{:S(2)}, u32[]{:S(2)}) %collective-permute-start.10) | collective-permute-done | bytes 65568 | tf_op jit(solution)/shard_map/ppermute | solution.py:29
  38.6 2.5 %collective-permute-done.11.refs_3_ = bf16[128,256]{1,0:T(8,128)(2,1)S(1)} collective-permute-done((bf16[128,256]{1,0:T(8,128)(2,1)S(1)}, bf16[128,256]{1,0:T(8,128)(2,1)S(1)}, u32[]{:S(2)}, u32[]{:S(2)}) %collective-permute-start.11) | collective-permute-done | bytes 65568 | tf_op jit(solution)/shard_map/ppermute | solution.py:29
  41.1 0.6 %collective-permute-done.9.refs_1_ = bf16[128,256]{1,0:T(8,128)(2,1)S(1)} collective-permute-done((bf16[128,256]{1,0:T(8,128)(2,1)S(1)}, bf16[128,256]{1,0:T(8,128)(2,1)S(1)}, u32[]{:S(2)}, u32[]{:S(2)}) %collective-permute-start.9) | collective-permute-done | bytes 65568 | tf_op jit(solution)/shard_map/ppermute | solution.py:29
  41.7 0.2 shard_map.134
  41.9 0.1 collective-permute-start.12
  42.0 1.2 %collective-permute-done.12.sq_b = f32[8,128]{1,0:T(8,128)S(1)} collective-permute-done((f32[8,128]{1,0:T(8,128)S(1)}, f32[8,128]{1,0:T(8,128)S(1)}, u32[]{:S(2)}, u32[]{:S(2)}) %collective-permute-start.12) | collective-permute-done | bytes 4128 | tf_op jit(solution)/shard_map/ppermute | solution.py:29
  43.2 0.0 collective-permute-done.16.st_far
  43.2 2.0 %shard_map.135 = (bf16[128,2048]{1,0:T(8,128)(2,1)}, f32[16,1,128]{2,1,0:T(1,128)}, f32[16,1,128]{2,1,0:T(1,128)}, f32[16,1,128]{2,1,0:T(1,128)}) custom-call(bf16[128,2048]{1,0:T(8,128)(2,1)S(1)} %shard_map.129.refs_0_.q, f32[2048,128]{1,0:T(8,128)S(1)} %get-tuple-element.29.acc_in, f32[2048,128]{1,0:T(8,128)S(1)} %get-tuple-element.30.total_in, ...), custom_call_target="tpu_custom_call" | custom-call | tf_op jit(solution)/shard_map/pallas_call | solution.py:374
  (5 shorter events, 0.1 us)
Async XLA Ops:
  1.5 6.0 %collective-permute-start.13 = (f32[48,128]{1,0:T(8,128)S(1)}, f32[48,128]{1,0:T(8,128)S(1)}, u32[]{:S(2)}, u32[]{:S(2)}) collective-permute-start(f32[48,128]{1,0:T(8,128)S(1)} %get-tuple-element.35), channel_id=1, source_target_pairs={{0,8},{2,10},{4,12},{6,14},{8,0},{10,2},{12,4},{14,6},{1,9},{3,11}... | collective-permute-start | bytes 73736 | tf_op jit(solution)/shard_map/ppermute | solution.py:29
  5.7 6.0 %collective-permute-start = (bf16[304,128]{1,0:T(8,128)(2,1)S(1)}, bf16[304,128]{1,0:T(8,128)(2,1)S(1)}, u32[]{:S(2)}, u32[]{:S(2)}) collective-permute-start(bf16[304,128]{1,0:T(8,128)(2,1)S(1)} %get-tuple-element.22.refs_1_.refs_2_.refs_5_), channel_id=1, source_target_pairs={{0,8},{2,10},{4,12},{6,14},{8,0},{10,2},{12,4},{14,6},{1,9},{3,11}... | collective-permute-start | bytes 233480 | tf_op jit(solution)/shard_map/ppermute | solution.py:29
  5.7 5.9 %collective-permute-start.2 = (bf16[304,128]{1,0:T(8,128)(2,1)S(1)}, bf16[304,128]{1,0:T(8,128)(2,1)S(1)}, u32[]{:S(2)}, u32[]{:S(2)}) collective-permute-start(bf16[304,128]{1,0:T(8,128)(2,1)S(1)} %get-tuple-element.22.refs_1_.refs_2_.refs_5_), channel_id=1, source_target_pairs={{0,4},{2,6},{4,0},{6,2},{8,12},{10,14},{12,8},{14,10},{1,5},{3,7},... | collective-permute-start | bytes 233480 | tf_op jit(solution)/shard_map/ppermute | solution.py:29
  7.6 6.8 %collective-permute-start.14 = (f32[96,128]{1,0:T(8,128)S(1)}, f32[96,128]{1,0:T(8,128)S(1)}, u32[]{:S(2)}, u32[]{:S(2)}) collective-permute-start(f32[96,128]{1,0:T(8,128)S(1)} %pad_maximum_fusion.3), channel_id=1, source_target_pairs={{0,16},{16,0},{1,17},{17,1},{2,18},{18,2},{3,19},{19,3},{4,20},{20... | collective-permute-start | bytes 147464 | tf_op jit(solution)/shard_map/ppermute | solution.py:29
  11.7 9.8 %collective-permute-start.3 = (bf16[608,128]{1,0:T(8,128)(2,1)S(1)}, bf16[608,128]{1,0:T(8,128)(2,1)S(1)}, u32[]{:S(2)}, u32[]{:S(2)}) collective-permute-start(bf16[608,128]{1,0:T(8,128)(2,1)S(1)} %pad_maximum_fusion.1), channel_id=1, source_target_pairs={{0,2},{2,0},{4,6},{6,4},{8,10},{10,8},{12,14},{14,12},{1,3},{3,1},... | collective-permute-start | bytes 466952 | tf_op jit(solution)/shard_map/ppermute | solution.py:29
  13.2 4.4 %collective-permute-start.1 = (bf16[304,128]{1,0:T(8,128)(2,1)S(1)}, bf16[304,128]{1,0:T(8,128)(2,1)S(1)}, u32[]{:S(2)}, u32[]{:S(2)}) collective-permute-start(bf16[304,128]{1,0:T(8,128)(2,1)S(1)} %collective-permute-done.refs_3_.refs_6_), channel_id=1, source_target_pairs={{0,4},{2,6},{4,0},{6,2},{8,12},{10,14},{12,8},{14,10},{1,5},{3,7},... | collective-permute-start | bytes 233480 | tf_op jit(solution)/shard_map/ppermute | solution.py:29
  14.4 15.4 %collective-permute-start.15 = (f32[192,128]{1,0:T(8,128)S(1)}, f32[192,128]{1,0:T(8,128)S(1)}, u32[]{:S(2)}, u32[]{:S(2)}) collective-permute-start(f32[192,128]{1,0:T(8,128)S(1)} %pad_maximum_fusion.2), channel_id=1, source_target_pairs={{0,4},{2,6},{4,0},{6,2},{8,12},{10,14},{12,8},{14,10},{1,5},{3,7},... | collective-permute-start | bytes 294920 | tf_op jit(solution)/shard_map/ppermute | solution.py:29
  15.4 4.4 %collective-permute-start.4 = (bf16[304,128]{1,0:T(8,128)(2,1)S(1)}, bf16[304,128]{1,0:T(8,128)(2,1)S(1)}, u32[]{:S(2)}, u32[]{:S(2)}) collective-permute-start(bf16[304,128]{1,0:T(8,128)(2,1)S(1)} %get-tuple-element.22.refs_1_.refs_2_.refs_5_), channel_id=1, source_target_pairs={{0,2},{2,0},{4,6},{6,4},{8,10},{10,8},{12,14},{14,12},{1,3},{3,1},... | collective-permute-start | bytes 233480 | tf_op jit(solution)/shard_map/ppermute | solution.py:29
  17.6 5.1 %collective-permute-start.5 = (bf16[304,128]{1,0:T(8,128)(2,1)S(1)}, bf16[304,128]{1,0:T(8,128)(2,1)S(1)}, u32[]{:S(2)}, u32[]{:S(2)}) collective-permute-start(bf16[304,128]{1,0:T(8,128)(2,1)S(1)} %collective-permute-done.1.refs_2_.refs_8_), channel_id=1, source_target_pairs={{0,2},{2,0},{4,6},{6,4},{8,10},{10,8},{12,14},{14,12},{1,3},{3,1},... | collective-permute-start | bytes 233480 | tf_op jit(solution)/shard_map/ppermute | solution.py:29
  21.5 1.3 %copy-start = (bf16[1,128,2048]{2,1,0:T(8,128)(2,1)S(1)}, bf16[1,128,2048]{2,1,0:T(8,128)(2,1)}, u32[]{:S(2)}) copy-start(bf16[1,128,2048]{2,1,0:T(8,128)(2,1)} %param.11) | copy-start | bytes 1572868
  25.4 6.2 %collective-permute-start.6 = (bf16[128,256]{1,0:T(8,128)(2,1)S(1)}, bf16[128,256]{1,0:T(8,128)(2,1)S(1)}, u32[]{:S(2)}, u32[]{:S(2)}) collective-permute-start(bf16[128,256]{1,0:T(8,128)(2,1)S(1)} %get-tuple-element.32), channel_id=1, source_target_pairs={{0,12},{2,14},{4,8},{6,10},{8,4},{10,6},{12,0},{14,2},{16,28},{18,... | collective-permute-start | bytes 196616 | tf_op jit(solution)/shard_map/ppermute | solution.py:29
  29.1 5.2 %collective-permute-start.7 = (bf16[128,256]{1,0:T(8,128)(2,1)S(1)}, bf16[128,256]{1,0:T(8,128)(2,1)S(1)}, u32[]{:S(2)}, u32[]{:S(2)}) collective-permute-start(bf16[128,256]{1,0:T(8,128)(2,1)S(1)} %get-tuple-element.32), channel_id=1, source_target_pairs={{0,8},{2,10},{4,12},{6,14},{8,0},{10,2},{12,4},{14,6},{16,24},{18,... | collective-permute-start | bytes 196616 | tf_op jit(solution)/shard_map/ppermute | solution.py:29
  29.1 5.2 %collective-permute-start.8 = (bf16[128,256]{1,0:T(8,128)(2,1)S(1)}, bf16[128,256]{1,0:T(8,128)(2,1)S(1)}, u32[]{:S(2)}, u32[]{:S(2)}) collective-permute-start(bf16[128,256]{1,0:T(8,128)(2,1)S(1)} %get-tuple-element.32), channel_id=1, source_target_pairs={{0,4},{2,6},{4,0},{6,2},{8,12},{10,14},{12,8},{14,10},{16,20},{18,... | collective-permute-start | bytes 196616 | tf_op jit(solution)/shard_map/ppermute | solution.py:29
  29.8 13.3 %collective-permute-start.16 = (f32[384,128]{1,0:T(8,128)S(1)}, f32[384,128]{1,0:T(8,128)S(1)}, u32[]{:S(2)}, u32[]{:S(2)}) collective-permute-start(f32[384,128]{1,0:T(8,128)S(1)} %pad_maximum_fusion.st_near), channel_id=1, source_target_pairs={{0,2},{2,0},{4,6},{6,4},{8,10},{10,8},{12,14},{14,12},{1,3},{3,1},... | collective-permute-start | bytes 589832 | tf_op jit(solution)/shard_map/ppermute | solution.py:29
  34.3 4.3 %collective-permute-start.10 = (bf16[128,256]{1,0:T(8,128)(2,1)S(1)}, bf16[128,256]{1,0:T(8,128)(2,1)S(1)}, u32[]{:S(2)}, u32[]{:S(2)}) collective-permute-start(bf16[128,256]{1,0:T(8,128)(2,1)S(1)} %add_convert_fusion.refs_0_), channel_id=1, source_target_pairs={{0,16},{2,18},{4,20},{6,22},{8,24},{10,26},{12,28},{14,30},{16,0},... | collective-permute-start | bytes 196616 | tf_op jit(solution)/shard_map/ppermute | solution.py:29
  35.9 5.2 %collective-permute-start.11 = (bf16[128,256]{1,0:T(8,128)(2,1)S(1)}, bf16[128,256]{1,0:T(8,128)(2,1)S(1)}, u32[]{:S(2)}, u32[]{:S(2)}) collective-permute-start(bf16[128,256]{1,0:T(8,128)(2,1)S(1)} %add_convert_fusion.refs_0_), channel_id=1, source_target_pairs={{0,18},{2,16},{4,22},{6,20},{8,26},{10,24},{12,30},{14,28},{16,2},... | collective-permute-start | bytes 196616 | tf_op jit(solution)/shard_map/ppermute | solution.py:29
  36.9 4.9 %collective-permute-start.9 = (bf16[128,256]{1,0:T(8,128)(2,1)S(1)}, bf16[128,256]{1,0:T(8,128)(2,1)S(1)}, u32[]{:S(2)}, u32[]{:S(2)}) collective-permute-start(bf16[128,256]{1,0:T(8,128)(2,1)S(1)} %add_convert_fusion.refs_0_), channel_id=1, source_target_pairs={{0,2},{2,0},{4,6},{6,4},{8,10},{10,8},{12,14},{14,12},{16,18},{18,... | collective-permute-start | bytes 196616 | tf_op jit(solution)/shard_map/ppermute | solution.py:29
  41.9 1.2 %collective-permute-start.12 = (f32[8,128]{1,0:T(8,128)S(1)}, f32[8,128]{1,0:T(8,128)S(1)}, u32[]{:S(2)}, u32[]{:S(2)}) collective-permute-start(f32[8,128]{1,0:T(8,128)S(1)} %get-tuple-element.34.sq_a), channel_id=1, source_target_pairs={{0,1},{1,0},{2,3},{3,2},{4,5},{5,4},{6,7},{7,6},{8,9},{9,8},{10,11... | collective-permute-start | bytes 12296 | tf_op jit(solution)/shard_map/ppermute | solution.py:29
